TPU v7x, 256 devices: a whole 4x4x8 slice. The times are simulated.
256 devices in a mesh: row: 32 (over x, y, core), col: 8 (over z).
Axes of the slice: x: 4, y: 4, z: 8, core: 2. Of those that a mesh axis runs over, the one named last changes fastest.
Arguments:
- matrix: bfloat16 [65536, 8192], P('row', 'col'), may hold values from 0 to 1
- labels: int32 [65536, 1], P('row'), may hold values from 0 to 7
- root_rows: float32 [8, 65536], P(None, 'row'), may hold values from 0.2 to 1
- root_cols: float32 [8, 8192], P(None, 'col'), may hold values from 0.2 to 1
- child_rows: float32 [16, 65536], P(None, 'row'), may hold values from 0.2 to 1
- child_cols: float32 [128, 8192], P(None, 'col'), may hold values from 0.2 to 1
Outputs:
- root_w: float32 [8, 65536], P(None, 'row')
- root_h: float32 [8, 8192], P(None, 'col')
- child_w: float32 [16, 65536], P(None, 'row')
- child_h: float32 [128, 8192], P(None, 'col')
Inputs may be any that keep to these rules, and one draw needn't show every extreme that they name: `labels`: every cluster 0 to 7 holds at least one node.
All inputs are finite; a program needn't handle non-finite values.
Results may differ from a plain program's by a relative error of at most 0.00035.
Values sent between devices are 32-bit elements; how exact they have to be, the bound alone decides.
A program may use at most 64 MiB of HBM per device.

v0:
```python
import functools

import jax
import jax.numpy as jnp
from jax import lax
from jax.experimental import pallas as pl
from jax.experimental.pallas import tpu as pltpu
from jax.sharding import PartitionSpec as P

MESH = pl.DeviceIdType.MESH
F32, BF16 = jnp.float32, jnp.bfloat16
K_ROOT, K_CHILD, CHILDREN = 8, 16, 8
ROOT_ITERS, CHILD_ITERS = 2, 3
TOTAL = CHILDREN * K_CHILD
NODES, BINS, HALF = 2048, 1024, 512
ZN, CHUNK = 8, 256
CHIPS = 16


def ring(d, n):
    return min(d, n - d)


XY = sorted(
    [(dx, dy) for dx in range(4) for dy in range(4) if dx or dy],
    key=lambda o: -(ring(o[0], 4) + ring(o[1], 4)),
)
XY_ARRIVAL = list(reversed(range(len(XY))))
Z_SEND = [4, 3, 5, 2, 6, 1, 7]
Z_ARRIVAL = [1, 7, 2, 6, 3, 5, 4]


def nn(a, b):
    return jnp.dot(a, b, preferred_element_type=F32)


def nt(a, b):
    return lax.dot_general(a, b, (((1,), (1,)), ((), ())), preferred_element_type=F32)


def parts(a):
    high = a.astype(BF16)
    return high, (a - high.astype(F32)).astype(BF16)


def gram3(high, low):
    return nt(high, high) + (nt(high, low) + nt(low, high))


def padded(gram):
    rows, cols = gram.shape
    return jnp.concatenate([gram, jnp.zeros((rows, 128 - cols), F32)], axis=1)


def small_product(gram, rows, count):
    total = gram[:, 0:1] * rows[0:1, :]
    for k in range(1, count):
        total = total + gram[:, k : k + 1] * rows[k : k + 1, :]
    return total


def kernel(
    x_hbm, lab_ref, rr_ref, rc_hbm, cr_ref, cc_hbm,
    o_rw, o_rh, o_cw, o_ch,
    xv, cc, lb, crv, rh, rw, cw, hb, hbb, acc, no, gacc,
    rxs, rxr, fr, zs_r, zr_r,
    nps, cxr, gxs, gxr, rss, rsr, zs_c, zr_c,
    in_sem, out_sem,
    s_rx, r_rx, s_fr, r_fr, s_rh, r_rh, s_zr, r_zr, s_rw, r_rw,
    s_cx, r_cx, s_rs, r_rs, s_ag, r_ag, s_re, r_re, s_zc, r_zc, s_cw, r_cw,
):
    row, z = lax.axis_index("row"), lax.axis_index("col")
    p, core = lax.div(row, 2), lax.rem(row, 2)
    x, y = lax.div(p, 4), lax.rem(p, 4)
    child = lax.div(p, 2)

    def chip(dx, dy):
        return lax.rem(x + dx + 4, 4) * 4 + lax.rem(y + dy + 4, 4)

    def xy_peer(o):
        return {"row": chip(*o) * 2 + core, "col": z}

    def z_at(d):
        return lax.rem(z + d + ZN, ZN)

    def z_peer(d):
        return {"row": row, "col": z_at(d)}

    partner = {"row": p * 2 + 1 - core, "col": z}
    pending = []

    def send(src, dst, ssem, rsem, device):
        copy = pltpu.make_async_remote_copy(
            src_ref=src, dst_ref=dst, send_sem=ssem, recv_sem=rsem,
            device_id=device, device_id_type=MESH,
        )
        copy.start()
        pending.append(copy)
        return copy

    def flush(keep):
        while len(pending) > keep:
            pending.pop(0).wait_send()

    loads = []
    for half in range(2):
        first = pl.multiple_of(HALF * (core if half == 0 else 1 - core), HALF)
        for i in range(4):
            rows = pl.ds(i * 512, 512)
            loads.append(
                pltpu.make_async_copy(
                    x_hbm.at[rows, pl.ds(first, HALF)], xv.at[half, rows], in_sem.at[half * 4 + i]
                )
            )
    own_cols = pl.ds(pl.multiple_of(HALF * core, HALF), HALF)
    other_cols = pl.ds(pl.multiple_of(HALF * (1 - core), HALF), HALF)
    load_cc = pltpu.make_async_copy(
        cc_hbm.at[pl.ds(pl.multiple_of(child * K_CHILD, 16), K_CHILD), own_cols], cc, in_sem.at[8]
    )
    load_rc = pltpu.make_async_copy(rc_hbm.at[:, own_cols], rh.at[0, 0], in_sem.at[9])
    for load in loads:
        load.start()
    load_rc.start()
    load_cc.start()

    barrier = pltpu.get_barrier_semaphore()
    pl.semaphore_signal(barrier, inc=1, device_id=partner, device_id_type=MESH)
    for o in XY:
        pl.semaphore_signal(barrier, inc=1, device_id=xy_peer(o), device_id_type=MESH)
    for d in Z_SEND:
        pl.semaphore_signal(barrier, inc=1, device_id=z_peer(d), device_id_type=MESH)

    for i in range(ZN):
        cols = slice(i * CHUNK, (i + 1) * CHUNK)
        rw[0, i] = rr_ref[:, cols]
        crv[i] = cr_ref[:, cols]
        lb[i] = jnp.broadcast_to(lab_ref[:, cols], (K_CHILD, CHUNK))

    def chunk_rows(zz):
        return pl.ds(pl.multiple_of(zz * CHUNK, CHUNK), CHUNK)

    def x_chunk(half, zz):
        return xv[half, chunk_rows(zz), :]

    for load in loads:
        load.wait()
    load_rc.wait()
    load_cc.wait()
    pl.semaphore_wait(barrier, 1 + len(XY) + len(Z_SEND))

    ag_w = None
    for it in range(ROOT_ITERS):
        mine = other = gram = None
        for d in [0] + Z_ARRIVAL:
            if it == 0:
                zz = z_at(d)
            else:
                zz = z_at(-d)
                if d:
                    ag_w[d].wait_recv()
            w = rw[it, zz]
            high, low = parts(w)
            other_d = nn(high, x_chunk(1, zz))
            mine_d = nn(high, x_chunk(0, zz))
            gram_d = gram3(high, low)
            other = other_d if other is None else other + other_d
            mine = mine_d if mine is None else mine + mine_d
            gram = gram_d if gram is None else gram + gram_d
        gram = padded(gram)
        rxs[it, :, 0:HALF] = other
        rxs[it, :, HALF:] = gram
        swap = send(rxs.at[it], rxr.at[it], s_rx.at[it], r_rx.at[it], partner)
        flush(1)
        swap.wait_recv()
        fr[it, p, :, 0:HALF] = mine + rxr[it, :, 0:HALF]
        fr[it, p, :, HALF:] = gram + rxr[it, :, HALF:]
        copies = [
            send(fr.at[it, p], fr.at[it, p], s_fr.at[it, i], r_fr.at[it, i], xy_peer(o))
            for i, o in enumerate(XY)
        ]
        flush(len(copies))
        for i in XY_ARRIVAL:
            copies[i].wait_recv()
        total = fr[it, 0]
        for q in range(1, CHIPS):
            total = total + fr[it, q]
        h = rh[it, 0]
        lower = small_product(total[:, HALF : HALF + K_ROOT], h, K_ROOT)
        h = h * total[:, 0:HALF] / lower
        rh[it + 1, 0] = h
        swap = send(rh.at[it + 1, 0], rh.at[it + 1, 1], s_rh.at[it], r_rh.at[it], partner)
        flush(1)
        high, low = parts(h)
        owns = {d: nt(high, x_chunk(0, z_at(d))) for d in Z_SEND + [0]}
        gram = gram3(high, low)
        swap.wait_recv()
        high, low = parts(rh[it + 1, 1])
        gram = padded(gram + gram3(high, low))
        copies = {}
        for d in Z_SEND + [0]:
            zs_r[it, d, :, 0:CHUNK] = owns[d] + nt(high, x_chunk(1, z_at(d)))
            zs_r[it, d, :, CHUNK:] = gram
            if d:
                copies[d] = send(zs_r.at[it, d], zr_r.at[it, d], s_zr.at[it, d], r_zr.at[it, d], z_peer(d))
        flush(len(copies))
        total = zs_r[it, 0]
        for d in Z_ARRIVAL:
            copies[d].wait_recv()
            total = total + zr_r[it, d]
        w = rw[it, z]
        lower = small_product(total[:, CHUNK : CHUNK + K_ROOT], w, K_ROOT)
        rw[it + 1, z] = w * total[:, 0:CHUNK] / lower
        ag_w = {
            d: send(rw.at[it + 1, z], rw.at[it + 1, z], s_rw.at[it, d], r_rw.at[it, d], z_peer(d))
            for d in Z_SEND
        }

    own16 = pl.ds(pl.multiple_of(child * K_CHILD, 16), K_CHILD)
    own8 = pl.ds(pl.multiple_of(p * 8, 8), 8)
    hb[0, 0, own16, :] = cc[...] * rh[ROOT_ITERS, 0, pl.ds(child, 1), :]

    def spread_of(zz, w):
        label = lb[zz]
        return jnp.concatenate([jnp.where(label == c, w, 0.0) for c in range(CHILDREN)], axis=0)

    lane_child = lax.div(lax.broadcasted_iota(jnp.int32, (K_CHILD, TOTAL), 1), K_CHILD)

    def diagonal(full):
        out = jnp.where(lane_child == 0, full[0:K_CHILD], 0.0)
        for c in range(1, CHILDREN):
            out = out + jnp.where(lane_child == c, full[c * K_CHILD : (c + 1) * K_CHILD], 0.0)
        return out

    for it in range(CHILD_ITERS):
        order = [0] + Z_ARRIVAL
        for d in order:
            zz = z_at(-d)
            if d:
                ag_w[d].wait_recv()
            if it == 0:
                label = lb[zz, 0:K_ROOT]
                ids = lax.broadcasted_iota(jnp.int32, (K_ROOT, CHUNK), 0)
                own_weight = jnp.sum(jnp.where(label == ids, rw[ROOT_ITERS, zz], 0.0), axis=0, keepdims=True)
                w = crv[zz] * own_weight
                cw[0, zz] = w
            else:
                w = cw[it, zz]
            high, low = parts(spread_of(zz, w))
            if d == 0:
                nps[it] = nn(high, x_chunk(1, zz))
                gacc[...] = gram3(high, low)
                no[...] = nn(high, x_chunk(0, zz))
            else:
                nps[it] += nn(high, x_chunk(1, zz))
                if d == order[-1]:
                    swap = send(nps.at[it], cxr.at[it], s_cx.at[it, 0], r_cx.at[it, 0], partner)
                gacc[...] += gram3(high, low)
                if d == order[-1]:
                    full = gacc[...]
                    gram = full[0:K_CHILD]
                    for c in range(1, CHILDREN):
                        gram = gram + full[c * K_CHILD : (c + 1) * K_CHILD]
                    gxs[it] = gram
                    swap_g = send(gxs.at[it], gxr.at[it], s_cx.at[it, 1], r_cx.at[it, 1], partner)
                no[...] += nn(high, x_chunk(0, zz))
        flush(2)
        swap_g.wait_recv()
        gram = gram + gxr[it]
        for c in range(CHILDREN):
            turned = gram if c == 0 else pltpu.roll(gram, TOTAL - c * K_CHILD, 1)
            rss[it, 2 * c, :, HALF:] = turned[0:8]
            rss[it, 2 * c + 1, :, HALF:] = turned[8:16]
        swap.wait_recv()
        for q in range(CHIPS):
            rss[it, q, :, 0:HALF] = no[8 * q : 8 * q + 8, :] + cxr[it, 8 * q : 8 * q + 8, :]
        copies = [
            send(rss.at[it, chip(*o)], rsr.at[it, i], s_rs.at[it, i], r_rs.at[it, i], xy_peer(o))
            for i, o in enumerate(XY)
        ]
        flush(len(copies))
        total = rss[it, p]
        for i in XY_ARRIVAL:
            copies[i].wait_recv()
            total = total + rsr[it, i]
        lower = small_product(total[:, HALF : HALF + K_CHILD], hb[it, 0, own16, :], K_CHILD)
        hb[it + 1, 0, own8, :] = hb[it, 0, own8, :] * total[:, 0:HALF] / lower
        own_h = hb.at[it + 1, 0, own8]
        copies = [
            send(own_h, own_h, s_ag.at[it, i], r_ag.at[it, i], xy_peer(o)) for i, o in enumerate(XY)
        ]
        relays = [send(own_h, hb.at[it + 1, 1, own8], s_re.at[it, 15], r_re.at[it, 15], partner)]
        flush(len(copies) + 1)
        for i in XY_ARRIVAL:
            copies[i].wait_recv()
            dx, dy = XY[i]
            rows = pl.ds(pl.multiple_of(chip(-dx, -dy) * 8, 8), 8)
            relays.append(
                send(hb.at[it + 1, 0, rows], hb.at[it + 1, 1, rows], s_re.at[it, i], r_re.at[it, i], partner)
            )
        high, low = parts(hb[it + 1, 0])
        hbb[0] = high
        for d in Z_SEND + [0]:
            acc[d] = nt(hbb[0], x_chunk(0, z_at(d)))
        full = gram3(high, low)
        flush(len(relays))
        for relay in relays:
            relay.wait_recv()
        high, low = parts(hb[it + 1, 1])
        hbb[1] = high
        gram = diagonal(full + gram3(high, low))
        copies = {}
        for d in Z_SEND + [0]:
            zz = z_at(d)
            label = lb[zz]
            rows_all = acc[d] + nt(hbb[1], x_chunk(1, zz))
            numer = jnp.where(label == 0, rows_all[0:K_CHILD], 0.0)
            for c in range(1, CHILDREN):
                numer = numer + jnp.where(label == c, rows_all[c * K_CHILD : (c + 1) * K_CHILD], 0.0)
            zs_c[it, d, :, 0:CHUNK] = numer
            zs_c[it, d, :, CHUNK:] = gram
            if d:
                copies[d] = send(zs_c.at[it, d], zr_c.at[it, d], s_zc.at[it, d], r_zc.at[it, d], z_peer(d))
        flush(len(copies))
        w = cw[it, z]
        s_high, s_low = parts(spread_of(z, w))
        total = zs_c[it, 0]
        for d in Z_ARRIVAL:
            copies[d].wait_recv()
            total = total + zr_c[it, d]
        g_high, g_low = parts(total[:, CHUNK:])
        lower = nn(g_high, s_high) + (nn(g_high, s_low) + nn(g_low, s_high))
        cw[it + 1, z] = w * total[:, 0:CHUNK] / lower
        ag_w = {
            d: send(cw.at[it + 1, z], cw.at[it + 1, z], s_cw.at[it, d], r_cw.at[it, d], z_peer(d))
            for d in Z_SEND
        }

    outs = [
        pltpu.make_async_copy(hb.at[CHILD_ITERS, 0], o_ch.at[:, own_cols], out_sem.at[0]),
        pltpu.make_async_copy(hb.at[CHILD_ITERS, 1], o_ch.at[:, other_cols], out_sem.at[1]),
        pltpu.make_async_copy(rh.at[ROOT_ITERS, 0], o_rh.at[:, own_cols], out_sem.at[2]),
        pltpu.make_async_copy(rh.at[ROOT_ITERS, 1], o_rh.at[:, other_cols], out_sem.at[3]),
    ]
    for out in outs:
        out.start()
    for i in range(ZN):
        o_rw[:, i * CHUNK : (i + 1) * CHUNK] = rw[ROOT_ITERS, i]
    flush(0)
    for d in Z_ARRIVAL:
        ag_w[d].wait_recv()
    for i in range(ZN):
        o_cw[:, i * CHUNK : (i + 1) * CHUNK] = cw[CHILD_ITERS, i]
    for out in outs:
        out.wait()


def body(matrix, labels, root_rows, root_cols, child_rows, child_cols):
    vmem = pl.BlockSpec(memory_space=pltpu.VMEM)
    hbm = pl.BlockSpec(memory_space=pl.ANY)
    dma = pltpu.SemaphoreType.DMA
    r, c = ROOT_ITERS, CHILD_ITERS
    n = len(XY)

    def v(*shape, dtype=F32):
        return pltpu.VMEM(shape, dtype)

    scratch = [
        v(2, NODES, HALF, dtype=BF16), v(K_CHILD, HALF), v(ZN, K_CHILD, CHUNK, dtype=jnp.int32),
        v(ZN, K_CHILD, CHUNK), v(r + 1, 2, K_ROOT, HALF), v(r + 1, ZN, K_ROOT, CHUNK),
        v(c + 1, ZN, K_CHILD, CHUNK), v(c + 1, 2, TOTAL, HALF), v(2, TOTAL, HALF, dtype=BF16),
        v(ZN, TOTAL, CHUNK), v(TOTAL, HALF), v(TOTAL, TOTAL),
        v(r, K_ROOT, HALF + 128), v(r, K_ROOT, HALF + 128), v(r, CHIPS, K_ROOT, HALF + 128),
        v(r, ZN, K_ROOT, CHUNK + 128), v(r, ZN, K_ROOT, CHUNK + 128),
        v(c, TOTAL, HALF), v(c, TOTAL, HALF), v(c, K_CHILD, TOTAL), v(c, K_CHILD, TOTAL),
        v(c, CHIPS, 8, HALF + 128), v(c, n, 8, HALF + 128),
        v(c, ZN, K_CHILD, CHUNK + 128), v(c, ZN, K_CHILD, CHUNK + 128),
        dma((10,)), dma((4,)),
        dma((r,)), dma((r,)), dma((r, n)), dma((r, n)), dma((r,)), dma((r,)),
        dma((r, ZN)), dma((r, ZN)), dma((r, ZN)), dma((r, ZN)),
        dma((c, 2)), dma((c, 2)), dma((c, n)), dma((c, n)), dma((c, n)), dma((c, n)),
        dma((c, n + 1)), dma((c, n + 1)), dma((c, ZN)), dma((c, ZN)), dma((c, ZN)), dma((c, ZN)),
    ]
    return pl.pallas_call(
        kernel,
        out_shape=(
            jax.ShapeDtypeStruct((K_ROOT, NODES), F32),
            jax.ShapeDtypeStruct((K_ROOT, BINS), F32),
            jax.ShapeDtypeStruct((K_CHILD, NODES), F32),
            jax.ShapeDtypeStruct((TOTAL, BINS), F32),
        ),
        in_specs=[hbm, vmem, vmem, hbm, vmem, hbm],
        out_specs=(vmem, hbm, vmem, hbm),
        scratch_shapes=scratch,
        compiler_params=pltpu.CompilerParams(
            collective_id=0, has_side_effects=True, vmem_limit_bytes=63 * 1024 * 1024
        ),
        name="nmf",
    )(matrix, labels.reshape(1, NODES), root_rows, root_cols, child_rows, child_cols)


def solution(mesh):
    return jax.shard_map(
        body,
        mesh=mesh,
        in_specs=(
            P("row", "col"), P("row", None), P(None, "row"),
            P(None, "col"), P(None, "row"), P(None, "col"),
        ),
        out_specs=(P(None, "row"), P(None, "col"), P(None, "row"), P(None, "col")),
        check_vma=False,
    )
```

profile of v0, /device:TPU:1, one launch (start us, length us, event | category | flops | bytes accessed | tf_op | source)
XLA Modules:
  0.0 146.7 jit_solution(11785457763321288378)
XLA Ops:
  0.6 139.7 %nmf.1 = (f32[8,2048]{1,0:T(8,128)}, f32[8,1024]{1,0:T(8,128)}, f32[16,2048]{1,0:T(8,128)}, f32[128,1024]{1,0:T(8,128)}) custom-call(bf16[2048,1024]{1,0:T(8,128)(2,1)} %x_hbm.1, s32[1,2048]{1,0:T(1,128)} %bitcast.1, f32[8,2048]{1,0:T(8,128)} %rr_ref.1, f32[8,1024]{1,0:T(8,128)} %rc_hbm.1, f32[16,2048]{1,0:T(8,128)} %cr_ref.1, f32[128,1024]{1,0:T(8,128)} %cc_hbm.1), custom_call_target="tpu_custom_call" | custom-call | tf_op jit(solution)/shard_map/nmf/pallas_call | solution.py:383
  140.4 1.5 %copy.14 = f32[8,2048]{1,0:T(8,128)} copy(f32[8,2048]{1,0:T(8,128)} %get-tuple-element.8) | data formatting | bytes 131072
  141.9 1.4 copy.15
  143.2 1.6 %copy.16 = f32[16,2048]{1,0:T(8,128)} copy(f32[16,2048]{1,0:T(8,128)} %get-tuple-element.10) | data formatting | bytes 262144
  144.8 1.9 %copy.17 = f32[128,1024]{1,0:T(8,128)} copy(f32[128,1024]{1,0:T(8,128)} %get-tuple-element.11) | data formatting | bytes 1048576
where the time goes:
time: 147 us
  Pallas kernels  140 us (95%)
  local copies, waits for them, and re-layouts  6.3 us (4%)
    pallas_call x1, Pallas kernels, body(): pl.pallas_call(kernel, out_shape=(jax.ShapeDtypeStruct((K_ROOT, NODES), F...  140 us
    unnamed x4, local copies, waits for them, and re-layouts  6.3 us

commit v1 on v0

v1 whole, which is shorter than its diff:
```python
import jax
import jax.numpy as jnp
from jax import lax
from jax.experimental import pallas as pl
from jax.experimental.pallas import tpu as pltpu
from jax.sharding import PartitionSpec as P

MESH = pl.DeviceIdType.MESH
F32, BF16 = jnp.float32, jnp.bfloat16
K_ROOT, K_CHILD, CHILDREN = 8, 16, 8
ROOT_ITERS, CHILD_ITERS = 2, 3
TOTAL = CHILDREN * K_CHILD
NODES, BINS, HALF = 2048, 1024, 512
ZN, CHUNK = 8, 256
CHIPS = 16


def ring(d, n):
    return min(d, n - d)


XY = sorted(
    [(dx, dy) for dx in range(4) for dy in range(4) if dx or dy],
    key=lambda o: -(ring(o[0], 4) + ring(o[1], 4)),
)
XY_ARRIVAL = list(reversed(range(len(XY))))
Z_SEND = [(e, d) for d in (4, 3, 5, 2, 6, 1, 7) for e in (0, 1)] + [(1, 0)]
Z_ARRIVAL = [(1, 0)] + [(e, d) for d in (1, 7, 2, 6, 3, 5, 4) for e in (0, 1)]
GROUPS = [[(0, 0)], [(1, 0)]] + [[(0, d), (1, d)] for d in (1, 7, 2, 6, 3, 5, 4)]


def nn(a, b):
    return jnp.dot(a, b, preferred_element_type=F32)


def nt(a, b):
    return lax.dot_general(a, b, (((1,), (1,)), ((), ())), preferred_element_type=F32)


def parts(a):
    high = a.astype(BF16)
    return high, (a - high.astype(F32)).astype(BF16)


def gram3(high, low):
    return nt(high, high) + (nt(high, low) + nt(low, high))


def padded(gram):
    rows, cols = gram.shape
    return jnp.concatenate([gram, jnp.zeros((rows, 128 - cols), F32)], axis=1)


def small_product(gram, rows, count):
    total = gram[:, 0:1] * rows[0:1, :]
    for k in range(1, count):
        total = total + gram[:, k : k + 1] * rows[k : k + 1, :]
    return total


def plus(a, b):
    return b if a is None else a + b


def kernel(
    x_hbm, lab_ref, rr_ref, rc_hbm, cr_ref, cc_hbm,
    o_rw, o_rh, o_cw, o_ch,
    xv, xo, xs, xr, cc, lab_other, cr_other, lb, crv,
    rh, rh_other, rw, cw, hb, hb_other, hbb, no, gacc,
    rxs, rxr, fr, zs_r, zr_r, rss, rsr, zs_c, zr_c,
    in_sem, s_x, r_x, s_m, r_m,
    s_fr, r_fr, s_zr, r_zr, s_rw, r_rw, s_rs, r_rs, s_ag, r_ag, s_zc, r_zc, s_cw, r_cw,
):
    row, z = lax.axis_index("row"), lax.axis_index("col")
    p, core = lax.div(row, 2), lax.rem(row, 2)
    x, y = lax.div(p, 4), lax.rem(p, 4)
    child = lax.div(p, 2)

    def chip(dx, dy):
        return lax.rem(x + dx + 4, 4) * 4 + lax.rem(y + dy + 4, 4)

    def xy_peer(o):
        return {"row": chip(*o) * 2 + core, "col": z}

    def z_at(d):
        return lax.rem(z + d + ZN, ZN)

    def z_peer(ed):
        e, d = ed
        return {"row": p * 2 + (core if e == 0 else 1 - core), "col": z_at(d)}

    partner = z_peer((1, 0))
    pending = []

    def send(src, dst, ssem, rsem, device):
        copy = pltpu.make_async_remote_copy(
            src_ref=src, dst_ref=dst, send_sem=ssem, recv_sem=rsem,
            device_id=device, device_id_type=MESH,
        )
        copy.start()
        pending.append(copy)
        return copy

    def flush(keep):
        while len(pending) > keep:
            pending.pop(0).wait_send()

    own_cols = pl.ds(pl.multiple_of(HALF * core, HALF), HALF)
    other_cols = pl.ds(pl.multiple_of(HALF * (1 - core), HALF), HALF)
    loads = []
    for i in range(4):
        rows = pl.ds(i * 512, 512)
        loads.append(pltpu.make_async_copy(x_hbm.at[rows, other_cols], xo.at[rows], in_sem.at[2 * i]))
        loads.append(pltpu.make_async_copy(x_hbm.at[rows, own_cols], xv.at[0, rows], in_sem.at[2 * i + 1]))
    load_cc = pltpu.make_async_copy(
        cc_hbm.at[pl.ds(pl.multiple_of(child * K_CHILD, 16), K_CHILD), own_cols], cc, in_sem.at[8]
    )
    load_rc = pltpu.make_async_copy(rc_hbm.at[:, own_cols], rh.at[0], in_sem.at[9])
    for load in loads:
        load.start()
    load_rc.start()
    load_cc.start()

    barrier = pltpu.get_barrier_semaphore()
    for o in XY:
        pl.semaphore_signal(barrier, inc=1, device_id=xy_peer(o), device_id_type=MESH)
    for ed in Z_SEND:
        pl.semaphore_signal(barrier, inc=1, device_id=z_peer(ed), device_id_type=MESH)

    def cols_of(i):
        return slice(i * CHUNK, (i + 1) * CHUNK)

    for i in range(ZN):
        rw[0, 0, i] = rr_ref[:, cols_of(i)]
        crv[0, i] = cr_ref[:, cols_of(i)]
        lb[0, i] = jnp.broadcast_to(lab_ref[:, cols_of(i)], (K_CHILD, CHUNK))

    def x_chunk(e, zz):
        return xv[e, pl.ds(pl.multiple_of(zz * CHUNK, CHUNK), CHUNK), :]

    ag_w = None
    for it in range(ROOT_ITERS):
        mine = gram = None
        if it == 0:
            other = None
            for i in range(ZN):
                if i % 2 == 0:
                    loads[i].wait()
                    loads[i + 1].wait()
                rows = pl.ds(i * CHUNK, CHUNK)
                high, low = parts(rw[0, 0, i])
                other = plus(other, nn(high, xo[rows, :]))
                mine = plus(mine, nn(high, xv[0, rows, :]))
                gram = plus(gram, gram3(high, low))
            load_rc.wait()
            load_cc.wait()
            gram = padded(gram)
            rxs[:, 0:HALF] = other
            rxs[:, HALF:] = gram
            pl.semaphore_wait(barrier, len(XY) + len(Z_SEND))
            swap = send(rxs, rxr, s_m.at[0], r_m.at[0], partner)
            x_copies = []

            def pass_on(i):
                rows = pl.ds(i * CHUNK, CHUNK)
                xs[rows, :] = xo[rows, :].astype(F32)
                x_copies.append(send(xs.at[rows], xr.at[rows], s_x.at[i], r_x.at[i], partner))

            for i in range(3):
                pass_on(i)
            swap.wait_recv()
            mine = mine + rxr[:, 0:HALF]
            gram = gram + rxr[:, HALF:]
        else:
            for group in GROUPS:
                for e, d in group:
                    if (e, d) != (0, 0):
                        ag_w[e, d].wait_recv()
                    zz = z_at(-d)
                    high, low = parts(rw[it, e, zz])
                    mine = plus(mine, nn(high, x_chunk(e, zz)))
                    gram = plus(gram, gram3(high, low))
            gram = padded(gram)
        fr[it, p, :, 0:HALF] = mine
        fr[it, p, :, HALF:] = gram
        copies = [
            send(fr.at[it, p], fr.at[it, p], s_fr.at[it, i], r_fr.at[it, i], xy_peer(o))
            for i, o in enumerate(XY)
        ]
        if it == 0:
            for i in range(3, ZN):
                pass_on(i)
            small = [
                send(lab_ref, lab_other, s_m.at[1], r_m.at[1], partner),
                send(cr_ref, cr_other, s_m.at[2], r_m.at[2], partner),
            ]
            for i in range(ZN):
                x_copies[i].wait_recv()
                rows = pl.ds(i * CHUNK, CHUNK)
                xv[1, rows, :] = xr[rows, :].astype(BF16)
            for copy in small:
                copy.wait_recv()
            for i in range(ZN):
                crv[1, i] = cr_other[:, cols_of(i)]
                lb[1, i] = jnp.broadcast_to(lab_other[:, cols_of(i)], (K_CHILD, CHUNK))
        else:
            flush(len(copies))
        for i in XY_ARRIVAL:
            copies[i].wait_recv()
        total = fr[it, 0]
        for q in range(1, CHIPS):
            total = total + fr[it, q]
        h = rh[it]
        lower = small_product(total[:, HALF : HALF + K_ROOT], h, K_ROOT)
        h = h * total[:, 0:HALF] / lower
        rh[it + 1] = h
        high, low = parts(h)
        gram = padded(gram3(high, low))
        copies = {}
        for e, d in Z_SEND + [(0, 0)]:
            zs_r[it, e, d, :, 0:CHUNK] = nt(high, x_chunk(e, z_at(d)))
            zs_r[it, e, d, :, CHUNK:] = gram
            if (e, d) != (0, 0):
                copies[e, d] = send(
                    zs_r.at[it, e, d], zr_r.at[it, e, d], s_zr.at[it, e, d], r_zr.at[it, e, d], z_peer((e, d))
                )
        flush(len(copies))
        total = zs_r[it, 0, 0]
        for e, d in Z_ARRIVAL:
            copies[e, d].wait_recv()
            total = total + zr_r[it, e, d]
        w = rw[it, 0, z]
        lower = small_product(total[:, CHUNK : CHUNK + K_ROOT], w, K_ROOT)
        rw[it + 1, 0, z] = w * total[:, 0:CHUNK] / lower
        ag_w = {
            (e, d): send(
                rw.at[it + 1, 0, z], rw.at[it + 1, e, z], s_rw.at[it, e, d], r_rw.at[it, e, d], z_peer((e, d))
            )
            for e, d in Z_SEND
        }
    rh_swap = send(rh.at[ROOT_ITERS], rh_other, s_m.at[3], r_m.at[3], partner)

    own16 = pl.ds(pl.multiple_of(child * K_CHILD, 16), K_CHILD)
    own8 = pl.ds(pl.multiple_of(p * 8, 8), 8)
    hb[0, own16, :] = cc[...] * rh[ROOT_ITERS, pl.ds(child, 1), :]

    def spread_of(e, zz, w):
        label = lb[e, zz]
        return jnp.concatenate([jnp.where(label == c, w, 0.0) for c in range(CHILDREN)], axis=0)

    lane_child = lax.div(lax.broadcasted_iota(jnp.int32, (K_CHILD, TOTAL), 1), K_CHILD)

    def diagonal(full):
        out = None
        for c in range(CHILDREN):
            out = plus(out, jnp.where(lane_child == c, full[c * K_CHILD : (c + 1) * K_CHILD], 0.0))
        return out

    for it in range(CHILD_ITERS):
        for g, group in enumerate(GROUPS):
            numer = gram = None
            for e, d in group:
                zz = z_at(-d)
                if (e, d) != (0, 0):
                    ag_w[e, d].wait_recv()
                if it == 0:
                    label = lb[e, zz, 0:K_ROOT]
                    ids = lax.broadcasted_iota(jnp.int32, (K_ROOT, CHUNK), 0)
                    own_weight = jnp.sum(
                        jnp.where(label == ids, rw[ROOT_ITERS, e, zz], 0.0), axis=0, keepdims=True
                    )
                    w = crv[e, zz] * own_weight
                    cw[0, e, zz] = w
                else:
                    w = cw[it, e, zz]
                high, low = parts(spread_of(e, zz, w))
                numer = plus(numer, nn(high, x_chunk(e, zz)))
                both = jnp.concatenate([high, low], axis=0)
                gram = plus(gram, nt(both, jnp.concatenate(parts(w), axis=0)))
            if g == 0:
                no[...] = numer
                gacc[...] = gram
            elif g < len(GROUPS) - 1:
                no[...] += numer
                gacc[...] += gram
        numer = no[...] + numer
        gram = gacc[...] + gram
        gram = padded(
            gram[0:TOTAL, 0:K_CHILD] + (gram[0:TOTAL, K_CHILD:] + gram[TOTAL:, 0:K_CHILD])
        )
        for q in range(CHIPS):
            rss[it, q, :, 0:HALF] = numer[8 * q : 8 * q + 8]
            rss[it, q, :, HALF:] = gram[8 * q : 8 * q + 8]
        copies = [
            send(rss.at[it, chip(*o)], rsr.at[it, i], s_rs.at[it, i], r_rs.at[it, i], xy_peer(o))
            for i, o in enumerate(XY)
        ]
        flush(len(copies))
        total = rss[it, p]
        for i in XY_ARRIVAL:
            copies[i].wait_recv()
            total = total + rsr[it, i]
        lower = small_product(total[:, HALF : HALF + K_CHILD], hb[it, own16, :], K_CHILD)
        hb[it + 1, own8, :] = hb[it, own8, :] * total[:, 0:HALF] / lower
        own_h = hb.at[it + 1, own8]
        copies = [
            send(own_h, own_h, s_ag.at[it, i], r_ag.at[it, i], xy_peer(o)) for i, o in enumerate(XY)
        ]
        flush(len(copies))
        for i in XY_ARRIVAL:
            copies[i].wait_recv()
        if it == CHILD_ITERS - 1:
            hb_swap = send(hb.at[it + 1], hb_other, s_m.at[4], r_m.at[4], partner)
        high, low = parts(hb[it + 1])
        hbb[...] = high
        full = nt(jnp.concatenate([high, low], axis=0), high)
        gram = diagonal(full[0:TOTAL] + (full[TOTAL:] + full[TOTAL:].T))
        copies = {}
        for e, d in Z_SEND + [(0, 0)]:
            zz = z_at(d)
            label = lb[e, zz]
            rows_all = nt(hbb[...], x_chunk(e, zz))
            numer = None
            for c in range(CHILDREN):
                numer = plus(numer, jnp.where(label == c, rows_all[c * K_CHILD : (c + 1) * K_CHILD], 0.0))
            zs_c[it, e, d, :, 0:CHUNK] = numer
            zs_c[it, e, d, :, CHUNK:] = gram
            if (e, d) != (0, 0):
                copies[e, d] = send(
                    zs_c.at[it, e, d], zr_c.at[it, e, d], s_zc.at[it, e, d], r_zc.at[it, e, d], z_peer((e, d))
                )
        flush(len(copies))
        w = cw[it, 0, z]
        s_high, s_low = parts(spread_of(0, z, w))
        total = zs_c[it, 0, 0]
        for e, d in Z_ARRIVAL:
            copies[e, d].wait_recv()
            total = total + zr_c[it, e, d]
        g_high, g_low = parts(total[:, CHUNK:])
        lower = nn(g_high, s_high) + (nn(g_high, s_low) + nn(g_low, s_high))
        cw[it + 1, 0, z] = w * total[:, 0:CHUNK] / lower
        last = it == CHILD_ITERS - 1
        ag_w = {
            (e, d): send(
                cw.at[it + 1, 0, z], cw.at[it + 1, e, z], s_cw.at[it, e, d], r_cw.at[it, e, d], z_peer((e, d))
            )
            for e, d in Z_SEND
            if e == 0 or not last
        }

    rh_swap.wait_recv()
    o_rh[:, own_cols] = rh[ROOT_ITERS]
    o_rh[:, other_cols] = rh_other[...]
    hb_swap.wait_recv()
    o_ch[:, own_cols] = hb[CHILD_ITERS]
    o_ch[:, other_cols] = hb_other[...]
    for i in range(ZN):
        o_rw[:, cols_of(i)] = rw[ROOT_ITERS, 0, i]
    flush(0)
    for e, d in Z_ARRIVAL:
        if (e, d) in ag_w:
            ag_w[e, d].wait_recv()
    for i in range(ZN):
        o_cw[:, cols_of(i)] = cw[CHILD_ITERS, 0, i]


def put_out(*refs):
    sources, targets, sem = refs[:4], refs[4:8], refs[8]
    copies = [pltpu.make_async_copy(s, t, sem.at[i]) for i, (s, t) in enumerate(zip(sources, targets))]
    for copy in copies:
        copy.start()
    for copy in copies:
        copy.wait()


def body(matrix, labels, root_rows, root_cols, child_rows, child_cols):
    vmem = pl.BlockSpec(memory_space=pltpu.VMEM)
    hbm = pl.BlockSpec(memory_space=pltpu.HBM)
    dma = pltpu.SemaphoreType.DMA
    r, c = ROOT_ITERS, CHILD_ITERS
    n = len(XY)

    def v(*shape, dtype=F32):
        return pltpu.VMEM(shape, dtype)

    i32 = jnp.int32
    scratch = [
        v(2, NODES, HALF, dtype=BF16), v(NODES, HALF, dtype=BF16), v(NODES, HALF), v(NODES, HALF),
        v(K_CHILD, HALF), v(1, NODES, dtype=i32), v(K_CHILD, NODES),
        v(2, ZN, K_CHILD, CHUNK, dtype=i32), v(2, ZN, K_CHILD, CHUNK),
        v(r + 1, K_ROOT, HALF), v(K_ROOT, HALF), v(r + 1, 2, ZN, K_ROOT, CHUNK),
        v(c + 1, 2, ZN, K_CHILD, CHUNK), v(c + 1, TOTAL, HALF), v(TOTAL, HALF),
        v(TOTAL, HALF, dtype=BF16), v(TOTAL, HALF), v(2 * TOTAL, 2 * K_CHILD),
        v(K_ROOT, HALF + 128), v(K_ROOT, HALF + 128), v(r, CHIPS, K_ROOT, HALF + 128),
        v(r, 2, ZN, K_ROOT, CHUNK + 128), v(r, 2, ZN, K_ROOT, CHUNK + 128),
        v(c, CHIPS, 8, HALF + 128), v(c, n, 8, HALF + 128),
        v(c, 2, ZN, K_CHILD, CHUNK + 128), v(c, 2, ZN, K_CHILD, CHUNK + 128),
        dma((10,)), dma((ZN,)), dma((ZN,)), dma((5,)), dma((5,)),
        dma((r, n)), dma((r, n)), dma((r, 2, ZN)), dma((r, 2, ZN)), dma((r, 2, ZN)), dma((r, 2, ZN)),
        dma((c, n)), dma((c, n)), dma((c, n)), dma((c, n)),
        dma((c, 2, ZN)), dma((c, 2, ZN)), dma((c, 2, ZN)), dma((c, 2, ZN)),
    ]
    shapes = (
        jax.ShapeDtypeStruct((K_ROOT, NODES), F32),
        jax.ShapeDtypeStruct((K_ROOT, BINS), F32),
        jax.ShapeDtypeStruct((K_CHILD, NODES), F32),
        jax.ShapeDtypeStruct((TOTAL, BINS), F32),
    )
    outs = pl.pallas_call(
        kernel,
        out_shape=shapes,
        in_specs=[hbm, vmem, vmem, hbm, vmem, hbm],
        out_specs=(vmem,) * 4,
        scratch_shapes=scratch,
        compiler_params=pltpu.CompilerParams(
            collective_id=0, has_side_effects=True, vmem_limit_bytes=54000000
        ),
        name="nmf",
    )(matrix, labels.reshape(1, NODES), root_rows, root_cols, child_rows, child_cols)
    return pl.pallas_call(
        put_out,
        out_shape=shapes,
        in_specs=[vmem] * 4,
        out_specs=(hbm,) * 4,
        scratch_shapes=[dma((4,))],
        compiler_params=pltpu.CompilerParams(vmem_limit_bytes=4 * 1024 * 1024),
        name="put_out",
    )(*outs)


def solution(mesh):
    return jax.shard_map(
        body,
        mesh=mesh,
        in_specs=(
            P("row", "col"), P("row", None), P(None, "row"),
            P(None, "col"), P(None, "row"), P(None, "col"),
        ),
        out_specs=(P(None, "row"), P(None, "col"), P(None, "row"), P(None, "col")),
        check_vma=False,
    )
```

time: 147 us -> 158 us (1.075)
  Pallas kernels: 140 us -> 152 us
  local copies, waits for them, and re-layouts: 6.3 us -> 4.23 us
    pallas_call x1 -> x2, Pallas kernels: 140 us -> 152 us  [the longest x1 152 us: body(): pl.pallas_call(kernel, out_shape=shapes, in_specs=[hbm, vmem, vmem, hbm,...]
    unnamed x4 -> x10, local copies, waits for them, and re-layouts: 6.3 us -> 4.23 us
where the time goes in v1:
time: 158 us; the launch traced here: 157 us
  Pallas kernels  152 us (96%)
  local copies, waits for them, and re-layouts  4.23 us (3%)
    pallas_call x1, Pallas kernels, body(): pl.pallas_call(kernel, out_shape=shapes, in_specs=[hbm, vmem, vmem, hbm,...  152 us
    unnamed x10, local copies, waits for them, and re-layouts  4.23 us

profile of v1, /device:TPU:1, one launch (start us, length us, event | category | flops | bytes accessed | tf_op | source)
XLA Modules:
  0.0 157.5 jit_solution(17883284382407547613)
XLA Ops:
  0.6 0.0 copy-start
  0.6 1.0 copy-done
  1.7 0.0 copy-start.1
  1.7 0.9 copy-done.1
  2.6 0.0 copy-start.2
  2.6 0.8 copy-done.2
  3.4 0.0 copy-start.3
  3.4 0.8 copy-done.3
  4.2 0.0 copy-start.4
  4.2 0.7 copy-done.4
  4.9 151.5 %nmf.1 = (f32[8,2048]{1,0:T(8,128)S(1)}, f32[8,1024]{1,0:T(8,128)S(1)}, f32[16,2048]{1,0:T(8,128)S(1)}, f32[128,1024]{1,0:T(8,128)S(1)}) custom-call(bf16[2048,1024]{1,0:T(8,128)(2,1)} %x_hbm.1, s32[1,2048]{1,0:T(1,128)S(1)} %bitcast.1, f32[8,2048]{1,0:T(8,128)S(1)} %copy-done.2, f32[8,1024]{1,0:T(8,128)S(1)} %copy-done.3, f32[16,2048]{1,0:T(8,128)S(1)} %copy-done.1, ...), custom_call_target="tpu_custom_call" | custom-call | tf_op jit(solution)/shard_map/nmf/pallas_call | solution.py:409
  156.4 0.9 put_out.1
Async XLA Ops:
  0.6 1.0 copy-start
  1.7 0.9 copy-start.1
  2.6 0.8 copy-start.2
  3.4 0.8 copy-start.3
  4.2 0.7 copy-start.4

commit v2 on v1

--- a/solution.py
+++ b/solution.py
@@ -24,9 +24,9 @@
     key=lambda o: -(ring(o[0], 4) + ring(o[1], 4)),
 )
 XY_ARRIVAL = list(reversed(range(len(XY))))
-Z_SEND = [(e, d) for d in (4, 3, 5, 2, 6, 1, 7) for e in (0, 1)] + [(1, 0)]
-Z_ARRIVAL = [(1, 0)] + [(e, d) for d in (1, 7, 2, 6, 3, 5, 4) for e in (0, 1)]
-GROUPS = [[(0, 0)], [(1, 0)]] + [[(0, d), (1, d)] for d in (1, 7, 2, 6, 3, 5, 4)]
+Z_SEND = [4, 3, 5, 2, 6, 1, 7]
+Z_ARRIVAL = [1, 7, 2, 6, 3, 5, 4]
+GROUPS = [[(0, 0)]] + [[(0, d), (1, p)] for d, p in zip(Z_ARRIVAL, [0] + Z_ARRIVAL)] + [[(1, 4)]]
 
 
 def nn(a, b):
@@ -67,9 +67,9 @@
     o_rw, o_rh, o_cw, o_ch,
     xv, xo, xs, xr, cc, lab_other, cr_other, lb, crv,
     rh, rh_other, rw, cw, hb, hb_other, hbb, no, gacc,
-    rxs, rxr, fr, zs_r, zr_r, rss, rsr, zs_c, zr_c,
+    rxs, rxr, fr, zs_r, zr_r, rss, rsr, zs_c, zr_c, gxs, gxr,
     in_sem, s_x, r_x, s_m, r_m,
-    s_fr, r_fr, s_zr, r_zr, s_rw, r_rw, s_rs, r_rs, s_ag, r_ag, s_zc, r_zc, s_cw, r_cw,
+    s_fr, r_fr, s_zr, r_zr, s_rw, r_rw, s_rs, r_rs, s_ag, r_ag, s_zc, r_zc, s_cw, r_cw, s_g, r_g, out_sem,
 ):
     row, z = lax.axis_index("row"), lax.axis_index("col")
     p, core = lax.div(row, 2), lax.rem(row, 2)
@@ -85,11 +85,10 @@
     def z_at(d):
         return lax.rem(z + d + ZN, ZN)
 
-    def z_peer(ed):
-        e, d = ed
-        return {"row": p * 2 + (core if e == 0 else 1 - core), "col": z_at(d)}
-
-    partner = z_peer((1, 0))
+    def z_peer(d):
+        return {"row": row, "col": z_at(d)}
+
+    partner = {"row": p * 2 + 1 - core, "col": z}
     pending = []
 
     def send(src, dst, ssem, rsem, device):
@@ -124,8 +123,9 @@
     barrier = pltpu.get_barrier_semaphore()
     for o in XY:
         pl.semaphore_signal(barrier, inc=1, device_id=xy_peer(o), device_id_type=MESH)
-    for ed in Z_SEND:
-        pl.semaphore_signal(barrier, inc=1, device_id=z_peer(ed), device_id_type=MESH)
+    for d in Z_SEND:
+        pl.semaphore_signal(barrier, inc=1, device_id=z_peer(d), device_id_type=MESH)
+    pl.semaphore_signal(barrier, inc=1, device_id=partner, device_id_type=MESH)
 
     def cols_of(i):
         return slice(i * CHUNK, (i + 1) * CHUNK)
@@ -137,6 +137,27 @@
 
     def x_chunk(e, zz):
         return xv[e, pl.ds(pl.multiple_of(zz * CHUNK, CHUNK), CHUNK), :]
+
+    class Spread:
+        def __init__(self, ref, ssem, rsem):
+            self.ref, self.ssem, self.rsem = ref, ssem, rsem
+            own = ref.at[0, z]
+            self.along = {d: send(own, own, ssem.at[0, d], rsem.at[0, d], z_peer(d)) for d in Z_SEND}
+            self.across = {}
+            self.relay(0)
+
+        def relay(self, d):
+            zz = z_at(-d)
+            self.across[d] = send(
+                self.ref.at[0, zz], self.ref.at[1, zz], self.ssem.at[1, d], self.rsem.at[1, d], partner
+            )
+
+        def arrive(self, e, d):
+            if e == 1:
+                self.across[d].wait_recv()
+            elif d:
+                self.along[d].wait_recv()
+                self.relay(d)
 
     ag_w = None
     for it in range(ROOT_ITERS):
@@ -157,7 +178,7 @@
             gram = padded(gram)
             rxs[:, 0:HALF] = other
             rxs[:, HALF:] = gram
-            pl.semaphore_wait(barrier, len(XY) + len(Z_SEND))
+            pl.semaphore_wait(barrier, len(XY) + len(Z_SEND) + 1)
             swap = send(rxs, rxr, s_m.at[0], r_m.at[0], partner)
             x_copies = []
 
@@ -174,8 +195,7 @@
         else:
             for group in GROUPS:
                 for e, d in group:
-                    if (e, d) != (0, 0):
-                        ag_w[e, d].wait_recv()
+                    ag_w.arrive(e, d)
                     zz = z_at(-d)
                     high, low = parts(rw[it, e, zz])
                     mine = plus(mine, nn(high, x_chunk(e, zz)))
@@ -216,28 +236,29 @@
         rh[it + 1] = h
         high, low = parts(h)
         gram = padded(gram3(high, low))
-        copies = {}
-        for e, d in Z_SEND + [(0, 0)]:
-            zs_r[it, e, d, :, 0:CHUNK] = nt(high, x_chunk(e, z_at(d)))
-            zs_r[it, e, d, :, CHUNK:] = gram
-            if (e, d) != (0, 0):
-                copies[e, d] = send(
-                    zs_r.at[it, e, d], zr_r.at[it, e, d], s_zr.at[it, e, d], r_zr.at[it, e, d], z_peer((e, d))
+        across, copies = {}, {}
+        for d in Z_SEND + [0]:
+            zs_r[it, 1, d, :, 0:CHUNK] = nt(high, x_chunk(1, z_at(d)))
+            zs_r[it, 1, d, :, CHUNK:] = gram
+            across[d] = send(zs_r.at[it, 1, d], zr_r.at[it, 1, d], s_zr.at[it, 1, d], r_zr.at[it, 1, d], partner)
+        owns = [nt(high, x_chunk(0, z_at(d))) for d in Z_SEND + [0]]
+        for own, d in zip(owns, Z_SEND + [0]):
+            across[d].wait_recv()
+            zs_r[it, 0, d, :, 0:CHUNK] = own + zr_r[it, 1, d, :, 0:CHUNK]
+            zs_r[it, 0, d, :, CHUNK:] = gram + zr_r[it, 1, d, :, CHUNK:]
+            if d:
+                copies[d] = send(
+                    zs_r.at[it, 0, d], zr_r.at[it, 0, d], s_zr.at[it, 0, d], r_zr.at[it, 0, d], z_peer(d)
                 )
         flush(len(copies))
         total = zs_r[it, 0, 0]
-        for e, d in Z_ARRIVAL:
-            copies[e, d].wait_recv()
-            total = total + zr_r[it, e, d]
+        for d in Z_ARRIVAL:
+            copies[d].wait_recv()
+            total = total + zr_r[it, 0, d]
         w = rw[it, 0, z]
         lower = small_product(total[:, CHUNK : CHUNK + K_ROOT], w, K_ROOT)
         rw[it + 1, 0, z] = w * total[:, 0:CHUNK] / lower
-        ag_w = {
-            (e, d): send(
-                rw.at[it + 1, 0, z], rw.at[it + 1, e, z], s_rw.at[it, e, d], r_rw.at[it, e, d], z_peer((e, d))
-            )
-            for e, d in Z_SEND
-        }
+        ag_w = Spread(rw.at[it + 1], s_rw.at[it], r_rw.at[it])
     rh_swap = send(rh.at[ROOT_ITERS], rh_other, s_m.at[3], r_m.at[3], partner)
 
     own16 = pl.ds(pl.multiple_of(child * K_CHILD, 16), K_CHILD)
@@ -261,8 +282,7 @@
             numer = gram = None
             for e, d in group:
                 zz = z_at(-d)
-                if (e, d) != (0, 0):
-                    ag_w[e, d].wait_recv()
+                ag_w.arrive(e, d)
                 if it == 0:
                     label = lb[e, zz, 0:K_ROOT]
                     ids = lax.broadcasted_iota(jnp.int32, (K_ROOT, CHUNK), 0)
@@ -315,62 +335,91 @@
         hbb[...] = high
         full = nt(jnp.concatenate([high, low], axis=0), high)
         gram = diagonal(full[0:TOTAL] + (full[TOTAL:] + full[TOTAL:].T))
-        copies = {}
-        for e, d in Z_SEND + [(0, 0)]:
-            zz = z_at(d)
+        def numer_of(e, zz):
             label = lb[e, zz]
             rows_all = nt(hbb[...], x_chunk(e, zz))
             numer = None
             for c in range(CHILDREN):
                 numer = plus(numer, jnp.where(label == c, rows_all[c * K_CHILD : (c + 1) * K_CHILD], 0.0))
-            zs_c[it, e, d, :, 0:CHUNK] = numer
-            zs_c[it, e, d, :, CHUNK:] = gram
-            if (e, d) != (0, 0):
-                copies[e, d] = send(
-                    zs_c.at[it, e, d], zr_c.at[it, e, d], s_zc.at[it, e, d], r_zc.at[it, e, d], z_peer((e, d))
+            return numer
+
+        gxs[it] = gram
+        swap_g = send(gxs.at[it], gxr.at[it], s_g.at[it], r_g.at[it], partner)
+        across, copies = {}, {}
+        for d in Z_SEND + [0]:
+            zs_c[it, 1, d, :, 0:CHUNK] = numer_of(1, z_at(d))
+            across[d] = send(
+                zs_c.at[it, 1, d, :, 0:CHUNK], zr_c.at[it, 1, d, :, 0:CHUNK],
+                s_zc.at[it, 1, d], r_zc.at[it, 1, d], partner,
+            )
+        for d in Z_SEND + [0]:
+            numer = numer_of(0, z_at(d))
+            if d == Z_SEND[0]:
+                swap_g.wait_recv()
+                gram = gram + gxr[it]
+            across[d].wait_recv()
+            zs_c[it, 0, d, :, 0:CHUNK] = numer + zr_c[it, 1, d, :, 0:CHUNK]
+            zs_c[it, 0, d, :, CHUNK:] = gram
+            if d:
+                copies[d] = send(
+                    zs_c.at[it, 0, d], zr_c.at[it, 0, d], s_zc.at[it, 0, d], r_zc.at[it, 0, d], z_peer(d)
                 )
         flush(len(copies))
         w = cw[it, 0, z]
         s_high, s_low = parts(spread_of(0, z, w))
         total = zs_c[it, 0, 0]
-        for e, d in Z_ARRIVAL:
-            copies[e, d].wait_recv()
-            total = total + zr_c[it, e, d]
+        for d in Z_ARRIVAL:
+            copies[d].wait_recv()
+            total = total + zr_c[it, 0, d]
         g_high, g_low = parts(total[:, CHUNK:])
         lower = nn(g_high, s_high) + (nn(g_high, s_low) + nn(g_low, s_high))
         cw[it + 1, 0, z] = w * total[:, 0:CHUNK] / lower
-        last = it == CHILD_ITERS - 1
-        ag_w = {
-            (e, d): send(
-                cw.at[it + 1, 0, z], cw.at[it + 1, e, z], s_cw.at[it, e, d], r_cw.at[it, e, d], z_peer((e, d))
-            )
-            for e, d in Z_SEND
-            if e == 0 or not last
-        }
-
+        if it < CHILD_ITERS - 1:
+            ag_w = Spread(cw.at[it + 1], s_cw.at[it], r_cw.at[it])
+        else:
+            own_w = cw.at[it + 1, 0, z]
+            copies = {
+                d: send(own_w, own_w, s_cw.at[it, 0, d], r_cw.at[it, 0, d], z_peer(d)) for d in Z_SEND
+            }
+
+    outs = []
+
+    def put(src, dst):
+        copy = pltpu.make_async_copy(src, dst, out_sem.at[len(outs)])
+        copy.start()
+        outs.append(copy)
+
+    def chunk_cols(zz):
+        return pl.ds(pl.multiple_of(zz * CHUNK, CHUNK), CHUNK)
+
+    put(hb.at[CHILD_ITERS], o_ch.at[:, own_cols])
+    put(rh.at[ROOT_ITERS], o_rh.at[:, own_cols])
     rh_swap.wait_recv()
-    o_rh[:, own_cols] = rh[ROOT_ITERS]
-    o_rh[:, other_cols] = rh_other[...]
+    put(rh_other, o_rh.at[:, other_cols])
+    for i in range(ZN):
+        put(rw.at[ROOT_ITERS, 0, i], o_rw.at[:, cols_of(i)])
     hb_swap.wait_recv()
-    o_ch[:, own_cols] = hb[CHILD_ITERS]
-    o_ch[:, other_cols] = hb_other[...]
-    for i in range(ZN):
-        o_rw[:, cols_of(i)] = rw[ROOT_ITERS, 0, i]
+    put(hb_other, o_ch.at[:, other_cols])
+    put(own_w, o_cw.at[:, chunk_cols(z)])
     flush(0)
-    for e, d in Z_ARRIVAL:
-        if (e, d) in ag_w:
-            ag_w[e, d].wait_recv()
-    for i in range(ZN):
-        o_cw[:, cols_of(i)] = cw[CHILD_ITERS, 0, i]
+    for d in Z_ARRIVAL:
+        copies[d].wait_recv()
+        put(cw.at[CHILD_ITERS, 0, z_at(-d)], o_cw.at[:, chunk_cols(z_at(-d))])
+    for out in outs:
+        out.wait()
 
 
 def put_out(*refs):
-    sources, targets, sem = refs[:4], refs[4:8], refs[8]
-    copies = [pltpu.make_async_copy(s, t, sem.at[i]) for i, (s, t) in enumerate(zip(sources, targets))]
-    for copy in copies:
-        copy.start()
-    for copy in copies:
-        copy.wait()
+    sources, targets, held, sem = refs[:4], refs[4:8], refs[8:12], refs[12]
+    loads = [pltpu.make_async_copy(s, h, sem.at[i]) for i, (s, h) in enumerate(zip(sources, held))]
+    stores = [pltpu.make_async_copy(h, t, sem.at[4 + i]) for i, (h, t) in enumerate(zip(held, targets))]
+    for load in loads:
+        load.start()
+    for load, store in zip(loads, stores):
+        load.wait()
+        store.start()
+    for store in stores:
+        store.wait()
 
 
 def body(matrix, labels, root_rows, root_cols, child_rows, child_cols):
@@ -395,10 +444,11 @@
         v(r, 2, ZN, K_ROOT, CHUNK + 128), v(r, 2, ZN, K_ROOT, CHUNK + 128),
         v(c, CHIPS, 8, HALF + 128), v(c, n, 8, HALF + 128),
         v(c, 2, ZN, K_CHILD, CHUNK + 128), v(c, 2, ZN, K_CHILD, CHUNK + 128),
+        v(c, K_CHILD, TOTAL), v(c, K_CHILD, TOTAL),
         dma((10,)), dma((ZN,)), dma((ZN,)), dma((5,)), dma((5,)),
         dma((r, n)), dma((r, n)), dma((r, 2, ZN)), dma((r, 2, ZN)), dma((r, 2, ZN)), dma((r, 2, ZN)),
         dma((c, n)), dma((c, n)), dma((c, n)), dma((c, n)),
-        dma((c, 2, ZN)), dma((c, 2, ZN)), dma((c, 2, ZN)), dma((c, 2, ZN)),
+        dma((c, 2, ZN)), dma((c, 2, ZN)), dma((c, 2, ZN)), dma((c, 2, ZN)), dma((c,)), dma((c,)), dma((20,)),
     ]
     shapes = (
         jax.ShapeDtypeStruct((K_ROOT, NODES), F32),
@@ -410,20 +460,20 @@
         kernel,
         out_shape=shapes,
         in_specs=[hbm, vmem, vmem, hbm, vmem, hbm],
-        out_specs=(vmem,) * 4,
+        out_specs=(hbm,) * 4,
         scratch_shapes=scratch,
         compiler_params=pltpu.CompilerParams(
-            collective_id=0, has_side_effects=True, vmem_limit_bytes=54000000
+            collective_id=0, has_side_effects=True, vmem_limit_bytes=63 * 1024 * 1024
         ),
         name="nmf",
     )(matrix, labels.reshape(1, NODES), root_rows, root_cols, child_rows, child_cols)
     return pl.pallas_call(
         put_out,
         out_shape=shapes,
-        in_specs=[vmem] * 4,
+        in_specs=[hbm] * 4,
         out_specs=(hbm,) * 4,
-        scratch_shapes=[dma((4,))],
-        compiler_params=pltpu.CompilerParams(vmem_limit_bytes=4 * 1024 * 1024),
+        scratch_shapes=[v(*s.shape) for s in shapes] + [dma((8,))],
+        compiler_params=pltpu.CompilerParams(vmem_limit_bytes=63 * 1024 * 1024),
         name="put_out",
     )(*outs)
 

time: 158 us -> 149 us (0.943)
  Pallas kernels: 152 us -> 147 us
  local copies, waits for them, and re-layouts: 4.23 us -> 0 us
    pallas_call x1, Pallas kernels: 152 us -> 145 us  [body(): pl.pallas_call(kernel, out_shape=shapes, in_specs=[hbm, vmem, vmem, hbm,...]
    unnamed x10 -> x0, local copies, waits for them, and re-layouts: 4.23 us -> none
where the time goes in v2:
time: 149 us; the launch traced here: 148 us
  Pallas kernels  147 us (99%)
    pallas_call x1, Pallas kernels, body(): pl.pallas_call(kernel, out_shape=shapes, in_specs=[hbm, vmem, vmem, hbm,...  145 us

profile of v2, /device:TPU:1, one launch (start us, length us, event | category | flops | bytes accessed | tf_op | source)
XLA Modules:
  0.0 148.1 jit_solution(6491217286297738976)
XLA Ops:
  0.6 145.2 %nmf.1 = (f32[8,2048]{1,0:T(8,128)}, f32[8,1024]{1,0:T(8,128)}, f32[16,2048]{1,0:T(8,128)}, f32[128,1024]{1,0:T(8,128)}) custom-call(bf16[2048,1024]{1,0:T(8,128)(2,1)} %x_hbm.1, s32[1,2048]{1,0:T(1,128)} %bitcast.1, f32[8,2048]{1,0:T(8,128)} %rr_ref.1, f32[8,1024]{1,0:T(8,128)} %rc_hbm.1, f32[16,2048]{1,0:T(8,128)} %cr_ref.1, f32[128,1024]{1,0:T(8,128)} %cc_hbm.1), custom_call_target="tpu_custom_call" | custom-call | tf_op jit(solution)/shard_map/nmf/pallas_call | solution.py:459
  145.9 2.0 %put_out.1 = (f32[8,2048]{1,0:T(8,128)}, f32[8,1024]{1,0:T(8,128)}, f32[16,2048]{1,0:T(8,128)}, f32[128,1024]{1,0:T(8,128)}) custom-call(f32[8,2048]{1,0:T(8,128)} %get-tuple-element.8.refs_0_, f32[8,1024]{1,0:T(8,128)} %get-tuple-element.9.refs_1_, f32[16,2048]{1,0:T(8,128)} %get-tuple-element.10.refs_2_, f32[128,1024]{1,0:T(8,128)} %get-tuple-element.11.refs_3_), custom_call_target="tpu_custom_call" | custom-call | tf_op jit(solution)/shard_map/put_out/pallas_call | solution.py:470

commit v3 on v0

--- a/solution.py
+++ b/solution.py
@@ -1,5 +1,3 @@
-import functools
-
 import jax
 import jax.numpy as jnp
 from jax import lax
@@ -64,10 +62,11 @@
     o_rw, o_rh, o_cw, o_ch,
     xv, cc, lb, crv, rh, rw, cw, hb, hbb, acc, no, gacc,
     rxs, rxr, fr, zs_r, zr_r,
-    nps, cxr, gxs, gxr, rss, rsr, zs_c, zr_c,
+    nps, cxr, gxs, gxr, rss, rsr, zs_c, zr_c, gcs, gcr, ghs, ghr,
     in_sem, out_sem,
     s_rx, r_rx, s_fr, r_fr, s_rh, r_rh, s_zr, r_zr, s_rw, r_rw,
     s_cx, r_cx, s_rs, r_rs, s_ag, r_ag, s_re, r_re, s_zc, r_zc, s_cw, r_cw,
+    s_gc, r_gc, s_gh, r_gh, s_gx, r_gx,
 ):
     row, z = lax.axis_index("row"), lax.axis_index("col")
     p, core = lax.div(row, 2), lax.rem(row, 2)
@@ -137,23 +136,20 @@
         lb[i] = jnp.broadcast_to(lab_ref[:, cols], (K_CHILD, CHUNK))
 
     def chunk_rows(zz):
-        return pl.ds(pl.multiple_of(zz * CHUNK, CHUNK), CHUNK)
+        return pl.ds(zz * CHUNK if isinstance(zz, int) else pl.multiple_of(zz * CHUNK, CHUNK), CHUNK)
 
     def x_chunk(half, zz):
         return xv[half, chunk_rows(zz), :]
-
-    for load in loads:
-        load.wait()
-    load_rc.wait()
-    load_cc.wait()
-    pl.semaphore_wait(barrier, 1 + len(XY) + len(Z_SEND))
 
     ag_w = None
     for it in range(ROOT_ITERS):
         mine = other = gram = None
-        for d in [0] + Z_ARRIVAL:
+        for step, d in enumerate([0] + Z_ARRIVAL):
             if it == 0:
-                zz = z_at(d)
+                zz = step
+                if step % 2 == 0:
+                    loads[step // 2].wait()
+                    loads[4 + step // 2].wait()
             else:
                 zz = z_at(-d)
                 if d:
@@ -167,6 +163,10 @@
             mine = mine_d if mine is None else mine + mine_d
             gram = gram_d if gram is None else gram + gram_d
         gram = padded(gram)
+        if it == 0:
+            load_rc.wait()
+            load_cc.wait()
+            pl.semaphore_wait(barrier, 1 + len(XY) + len(Z_SEND))
         rxs[it, :, 0:HALF] = other
         rxs[it, :, HALF:] = gram
         swap = send(rxs.at[it], rxr.at[it], s_rx.at[it], r_rx.at[it], partner)
@@ -246,44 +246,51 @@
             else:
                 w = cw[it, zz]
             high, low = parts(spread_of(zz, w))
-            if d == 0:
-                nps[it] = nn(high, x_chunk(1, zz))
-                gacc[...] = gram3(high, low)
-                no[...] = nn(high, x_chunk(0, zz))
+            first, last = d == 0, d == order[-1]
+            numer = nn(high, x_chunk(1, zz))
+            nps[it] = numer if first else nps[it] + numer
+            if last:
+                swap = send(nps.at[it], cxr.at[it], s_cx.at[it, 0], r_cx.at[it, 0], partner)
+            gram = nt(jnp.concatenate([high, low], axis=0), jnp.concatenate(parts(w), axis=0))
+            gram = gram if first else gacc[...] + gram
+            if not last:
+                gacc[...] = gram
             else:
-                nps[it] += nn(high, x_chunk(1, zz))
-                if d == order[-1]:
-                    swap = send(nps.at[it], cxr.at[it], s_cx.at[it, 0], r_cx.at[it, 0], partner)
-                gacc[...] += gram3(high, low)
-                if d == order[-1]:
-                    full = gacc[...]
-                    gram = full[0:K_CHILD]
-                    for c in range(1, CHILDREN):
-                        gram = gram + full[c * K_CHILD : (c + 1) * K_CHILD]
-                    gxs[it] = gram
-                    swap_g = send(gxs.at[it], gxr.at[it], s_cx.at[it, 1], r_cx.at[it, 1], partner)
-                no[...] += nn(high, x_chunk(0, zz))
-        flush(2)
+                gcs[it] = padded(
+                    gram[0:TOTAL, 0:K_CHILD] + (gram[0:TOTAL, K_CHILD:] + gram[TOTAL:, 0:K_CHILD])
+                )
+                gcopies = []
+                for i, o in enumerate(XY):
+                    rows = pl.ds(pl.multiple_of(chip(*o) * 8, 8), 8)
+                    gcopies.append(
+                        send(gcs.at[it, rows], gcr.at[it, i], s_gc.at[it, i], r_gc.at[it, i], xy_peer(o))
+                    )
+            numer = nn(high, x_chunk(0, zz))
+            no[...] = numer if first else no[...] + numer
+        flush(1 + len(gcopies))
+        swap.wait_recv()
+        copies = []
+        for i, o in enumerate(XY):
+            q = chip(*o)
+            rows = pl.ds(pl.multiple_of(q * 8, 8), 8)
+            rss[it, q] = no[rows, :] + cxr[it, rows, :]
+            copies.append(send(rss.at[it, q], rsr.at[it, i], s_rs.at[it, i], r_rs.at[it, i], xy_peer(o)))
+        total = no[own8, :] + cxr[it, own8, :]
+        gram = gcs[it, own8, :]
+        for i in XY_ARRIVAL:
+            gcopies[i].wait_recv()
+            gram = gram + gcr[it, i]
+        gxs[it, 0] = gram
+        swap_g = send(gxs.at[it, 0], gxr.at[it, 0], s_cx.at[it, 1], r_cx.at[it, 1], partner)
+        flush(len(copies) + 1)
         swap_g.wait_recv()
-        gram = gram + gxr[it]
-        for c in range(CHILDREN):
-            turned = gram if c == 0 else pltpu.roll(gram, TOTAL - c * K_CHILD, 1)
-            rss[it, 2 * c, :, HALF:] = turned[0:8]
-            rss[it, 2 * c + 1, :, HALF:] = turned[8:16]
-        swap.wait_recv()
-        for q in range(CHIPS):
-            rss[it, q, :, 0:HALF] = no[8 * q : 8 * q + 8, :] + cxr[it, 8 * q : 8 * q + 8, :]
-        copies = [
-            send(rss.at[it, chip(*o)], rsr.at[it, i], s_rs.at[it, i], r_rs.at[it, i], xy_peer(o))
-            for i, o in enumerate(XY)
-        ]
-        flush(len(copies))
-        total = rss[it, p]
+        gram = gram + gxr[it, 0]
+        old16 = hb[it, 0, own16, :]
+        lower = small_product(gram[:, 0:K_CHILD], old16, K_CHILD)
         for i in XY_ARRIVAL:
             copies[i].wait_recv()
             total = total + rsr[it, i]
-        lower = small_product(total[:, HALF : HALF + K_CHILD], hb[it, 0, own16, :], K_CHILD)
-        hb[it + 1, 0, own8, :] = hb[it, 0, own8, :] * total[:, 0:HALF] / lower
+        hb[it + 1, 0, own8, :] = hb[it, 0, own8, :] * total / lower
         own_h = hb.at[it + 1, 0, own8]
         copies = [
             send(own_h, own_h, s_ag.at[it, i], r_ag.at[it, i], xy_peer(o)) for i, o in enumerate(XY)
@@ -299,15 +306,17 @@
             )
         high, low = parts(hb[it + 1, 0])
         hbb[0] = high
+        full = nt(jnp.concatenate([high, low], axis=0), high)
+        ghs[it] = diagonal(full[0:TOTAL] + (full[TOTAL:] + full[TOTAL:].T))
+        gcopies = {
+            d: send(ghs.at[it], ghr.at[it, d], s_gh.at[it, d], r_gh.at[it, d], z_peer(d)) for d in Z_SEND
+        }
         for d in Z_SEND + [0]:
             acc[d] = nt(hbb[0], x_chunk(0, z_at(d)))
-        full = gram3(high, low)
-        flush(len(relays))
+        flush(len(relays) + len(gcopies))
         for relay in relays:
             relay.wait_recv()
-        high, low = parts(hb[it + 1, 1])
-        hbb[1] = high
-        gram = diagonal(full + gram3(high, low))
+        hbb[1] = hb[it + 1, 1].astype(BF16)
         copies = {}
         for d in Z_SEND + [0]:
             zz = z_at(d)
@@ -316,42 +325,64 @@
             numer = jnp.where(label == 0, rows_all[0:K_CHILD], 0.0)
             for c in range(1, CHILDREN):
                 numer = numer + jnp.where(label == c, rows_all[c * K_CHILD : (c + 1) * K_CHILD], 0.0)
-            zs_c[it, d, :, 0:CHUNK] = numer
-            zs_c[it, d, :, CHUNK:] = gram
+            zs_c[it, d] = numer
             if d:
                 copies[d] = send(zs_c.at[it, d], zr_c.at[it, d], s_zc.at[it, d], r_zc.at[it, d], z_peer(d))
-        flush(len(copies))
+        gram = ghs[it]
+        for d in Z_ARRIVAL:
+            gcopies[d].wait_recv()
+            gram = gram + ghr[it, d]
+        gxs[it, 1:3] = gram.reshape(2, 8, TOTAL)
+        swap_g = send(gxs.at[it, 1:3], gxr.at[it, 1:3], s_gx.at[it], r_gx.at[it], partner)
+        flush(len(copies) + 1)
         w = cw[it, z]
         s_high, s_low = parts(spread_of(z, w))
+        swap_g.wait_recv()
+        g_high, g_low = parts(gram + gxr[it, 1:3].reshape(K_CHILD, TOTAL))
+        lower = nn(g_high, s_high) + (nn(g_high, s_low) + nn(g_low, s_high))
         total = zs_c[it, 0]
         for d in Z_ARRIVAL:
             copies[d].wait_recv()
             total = total + zr_c[it, d]
-        g_high, g_low = parts(total[:, CHUNK:])
-        lower = nn(g_high, s_high) + (nn(g_high, s_low) + nn(g_low, s_high))
-        cw[it + 1, z] = w * total[:, 0:CHUNK] / lower
+        cw[it + 1, z] = w * total / lower
         ag_w = {
             d: send(cw.at[it + 1, z], cw.at[it + 1, z], s_cw.at[it, d], r_cw.at[it, d], z_peer(d))
             for d in Z_SEND
         }
 
-    outs = [
-        pltpu.make_async_copy(hb.at[CHILD_ITERS, 0], o_ch.at[:, own_cols], out_sem.at[0]),
-        pltpu.make_async_copy(hb.at[CHILD_ITERS, 1], o_ch.at[:, other_cols], out_sem.at[1]),
-        pltpu.make_async_copy(rh.at[ROOT_ITERS, 0], o_rh.at[:, own_cols], out_sem.at[2]),
-        pltpu.make_async_copy(rh.at[ROOT_ITERS, 1], o_rh.at[:, other_cols], out_sem.at[3]),
-    ]
-    for out in outs:
-        out.start()
+    outs = []
+
+    def put(src, dst):
+        copy = pltpu.make_async_copy(src, dst, out_sem.at[len(outs)])
+        copy.start()
+        outs.append(copy)
+
+    put(hb.at[CHILD_ITERS, 0], o_ch.at[:, own_cols])
+    put(hb.at[CHILD_ITERS, 1], o_ch.at[:, other_cols])
+    put(rh.at[ROOT_ITERS, 0], o_rh.at[:, own_cols])
+    put(rh.at[ROOT_ITERS, 1], o_rh.at[:, other_cols])
     for i in range(ZN):
-        o_rw[:, i * CHUNK : (i + 1) * CHUNK] = rw[ROOT_ITERS, i]
+        put(rw.at[ROOT_ITERS, i], o_rw.at[:, i * CHUNK : (i + 1) * CHUNK])
+    put(cw.at[CHILD_ITERS, z], o_cw.at[:, chunk_rows(z)])
     flush(0)
     for d in Z_ARRIVAL:
         ag_w[d].wait_recv()
-    for i in range(ZN):
-        o_cw[:, i * CHUNK : (i + 1) * CHUNK] = cw[CHILD_ITERS, i]
+        put(cw.at[CHILD_ITERS, z_at(-d)], o_cw.at[:, chunk_rows(z_at(-d))])
     for out in outs:
         out.wait()
+
+
+def put_out(*refs):
+    sources, targets, held, sem = refs[:4], refs[4:8], refs[8:12], refs[12]
+    loads = [pltpu.make_async_copy(s, h, sem.at[i]) for i, (s, h) in enumerate(zip(sources, held))]
+    stores = [pltpu.make_async_copy(h, t, sem.at[4 + i]) for i, (h, t) in enumerate(zip(held, targets))]
+    for load in loads:
+        load.start()
+    for load, store in zip(loads, stores):
+        load.wait()
+        store.start()
+    for store in stores:
+        store.wait()
 
 
 def body(matrix, labels, root_rows, root_cols, child_rows, child_cols):
@@ -368,34 +399,46 @@
         v(2, NODES, HALF, dtype=BF16), v(K_CHILD, HALF), v(ZN, K_CHILD, CHUNK, dtype=jnp.int32),
         v(ZN, K_CHILD, CHUNK), v(r + 1, 2, K_ROOT, HALF), v(r + 1, ZN, K_ROOT, CHUNK),
         v(c + 1, ZN, K_CHILD, CHUNK), v(c + 1, 2, TOTAL, HALF), v(2, TOTAL, HALF, dtype=BF16),
-        v(ZN, TOTAL, CHUNK), v(TOTAL, HALF), v(TOTAL, TOTAL),
+        v(ZN, TOTAL, CHUNK), v(TOTAL, HALF), v(2 * TOTAL, 2 * K_CHILD),
         v(r, K_ROOT, HALF + 128), v(r, K_ROOT, HALF + 128), v(r, CHIPS, K_ROOT, HALF + 128),
         v(r, ZN, K_ROOT, CHUNK + 128), v(r, ZN, K_ROOT, CHUNK + 128),
-        v(c, TOTAL, HALF), v(c, TOTAL, HALF), v(c, K_CHILD, TOTAL), v(c, K_CHILD, TOTAL),
-        v(c, CHIPS, 8, HALF + 128), v(c, n, 8, HALF + 128),
-        v(c, ZN, K_CHILD, CHUNK + 128), v(c, ZN, K_CHILD, CHUNK + 128),
-        dma((10,)), dma((4,)),
+        v(c, TOTAL, HALF), v(c, TOTAL, HALF), v(c, 3, 8, TOTAL), v(c, 3, 8, TOTAL),
+        v(c, CHIPS, 8, HALF), v(c, n, 8, HALF),
+        v(c, ZN, K_CHILD, CHUNK), v(c, ZN, K_CHILD, CHUNK),
+        v(c, TOTAL, 128), v(c, n, 8, 128), v(c, K_CHILD, TOTAL), v(c, ZN, K_CHILD, TOTAL),
+        dma((10,)), dma((20,)),
         dma((r,)), dma((r,)), dma((r, n)), dma((r, n)), dma((r,)), dma((r,)),
         dma((r, ZN)), dma((r, ZN)), dma((r, ZN)), dma((r, ZN)),
         dma((c, 2)), dma((c, 2)), dma((c, n)), dma((c, n)), dma((c, n)), dma((c, n)),
         dma((c, n + 1)), dma((c, n + 1)), dma((c, ZN)), dma((c, ZN)), dma((c, ZN)), dma((c, ZN)),
+        dma((c, n)), dma((c, n)), dma((c, ZN)), dma((c, ZN)), dma((c,)), dma((c,)),
     ]
-    return pl.pallas_call(
+    shapes = (
+        jax.ShapeDtypeStruct((K_ROOT, NODES), F32),
+        jax.ShapeDtypeStruct((K_ROOT, BINS), F32),
+        jax.ShapeDtypeStruct((K_CHILD, NODES), F32),
+        jax.ShapeDtypeStruct((TOTAL, BINS), F32),
+    )
+    outs = pl.pallas_call(
         kernel,
-        out_shape=(
-            jax.ShapeDtypeStruct((K_ROOT, NODES), F32),
-            jax.ShapeDtypeStruct((K_ROOT, BINS), F32),
-            jax.ShapeDtypeStruct((K_CHILD, NODES), F32),
-            jax.ShapeDtypeStruct((TOTAL, BINS), F32),
-        ),
+        out_shape=shapes,
         in_specs=[hbm, vmem, vmem, hbm, vmem, hbm],
-        out_specs=(vmem, hbm, vmem, hbm),
+        out_specs=(hbm,) * 4,
         scratch_shapes=scratch,
         compiler_params=pltpu.CompilerParams(
             collective_id=0, has_side_effects=True, vmem_limit_bytes=63 * 1024 * 1024
         ),
         name="nmf",
     )(matrix, labels.reshape(1, NODES), root_rows, root_cols, child_rows, child_cols)
+    return pl.pallas_call(
+        put_out,
+        out_shape=shapes,
+        in_specs=[hbm] * 4,
+        out_specs=(hbm,) * 4,
+        scratch_shapes=[v(*s.shape) for s in shapes] + [dma((8,))],
+        compiler_params=pltpu.CompilerParams(vmem_limit_bytes=63 * 1024 * 1024),
+        name="put_out",
+    )(*outs)
 
 
 def solution(mesh):

time: 147 us -> 139 us (0.946)
  local copies, waits for them, and re-layouts: 6.3 us -> 0 us
  Pallas kernels: 140 us -> 138 us
    unnamed x4 -> x0, local copies, waits for them, and re-layouts: 6.3 us -> none
    pallas_call x1 -> x2, Pallas kernels: 140 us -> 138 us  [the longest x1 136 us: body(): pl.pallas_call(kernel, out_shape=shapes, in_specs=[hbm, vmem, vmem, hbm,...]
where the time goes in v3:
time: 139 us; the launch traced here: 138 us
  Pallas kernels  138 us (99%)
    pallas_call x1, Pallas kernels, body(): pl.pallas_call(kernel, out_shape=shapes, in_specs=[hbm, vmem, vmem, hbm,...  136 us

profile of v3, /device:TPU:1, one launch (start us, length us, event | category | flops | bytes accessed | tf_op | source)
XLA Modules:
  0.0 138.5 jit_solution(14916844853591291919)
XLA Ops:
  0.6 135.6 %nmf.1 = (f32[8,2048]{1,0:T(8,128)}, f32[8,1024]{1,0:T(8,128)}, f32[16,2048]{1,0:T(8,128)}, f32[128,1024]{1,0:T(8,128)}) custom-call(bf16[2048,1024]{1,0:T(8,128)(2,1)} %x_hbm.1, s32[1,2048]{1,0:T(1,128)} %bitcast.1, f32[8,2048]{1,0:T(8,128)} %rr_ref.1, f32[8,1024]{1,0:T(8,128)} %rc_hbm.1, f32[16,2048]{1,0:T(8,128)} %cr_ref.1, f32[128,1024]{1,0:T(8,128)} %cc_hbm.1), custom_call_target="tpu_custom_call" | custom-call | tf_op jit(solution)/shard_map/nmf/pallas_call | solution.py:422
  136.3 2.0 %put_out.1 = (f32[8,2048]{1,0:T(8,128)}, f32[8,1024]{1,0:T(8,128)}, f32[16,2048]{1,0:T(8,128)}, f32[128,1024]{1,0:T(8,128)}) custom-call(f32[8,2048]{1,0:T(8,128)} %get-tuple-element.8.refs_0_, f32[8,1024]{1,0:T(8,128)} %get-tuple-element.9.refs_1_, f32[16,2048]{1,0:T(8,128)} %get-tuple-element.10.refs_2_, f32[128,1024]{1,0:T(8,128)} %get-tuple-element.11.refs_3_), custom_call_target="tpu_custom_call" | custom-call | tf_op jit(solution)/shard_map/put_out/pallas_call | solution.py:433

commit v4 on v3

--- a/solution.py
+++ b/solution.py
@@ -26,6 +26,7 @@
 XY_ARRIVAL = list(reversed(range(len(XY))))
 Z_SEND = [4, 3, 5, 2, 6, 1, 7]
 Z_ARRIVAL = [1, 7, 2, 6, 3, 5, 4]
+Z_GROUPS = [[0], [1, 7], [2, 6], [3, 5], [4]]
 
 
 def nn(a, b):
@@ -48,6 +49,10 @@
 def padded(gram):
     rows, cols = gram.shape
     return jnp.concatenate([gram, jnp.zeros((rows, 128 - cols), F32)], axis=1)
+
+
+def plus(a, b):
+    return b if a is None else a + b
 
 
 def small_product(gram, rows, count):
@@ -61,12 +66,12 @@
     x_hbm, lab_ref, rr_ref, rc_hbm, cr_ref, cc_hbm,
     o_rw, o_rh, o_cw, o_ch,
     xv, cc, lb, crv, rh, rw, cw, hb, hbb, acc, no, gacc,
-    rxs, rxr, fr, zs_r, zr_r,
+    rxs, rxr, fr, gfr, gfs, gft, zs_r, zr_r,
     nps, cxr, gxs, gxr, rss, rsr, zs_c, zr_c, gcs, gcr, ghs, ghr,
     in_sem, out_sem,
     s_rx, r_rx, s_fr, r_fr, s_rh, r_rh, s_zr, r_zr, s_rw, r_rw,
     s_cx, r_cx, s_rs, r_rs, s_ag, r_ag, s_re, r_re, s_zc, r_zc, s_cw, r_cw,
-    s_gc, r_gc, s_gh, r_gh, s_gx, r_gx,
+    s_gc, r_gc, s_gh, r_gh, s_gx, r_gx, s_gf, r_gf, s_gt, r_gt,
 ):
     row, z = lax.axis_index("row"), lax.axis_index("col")
     p, core = lax.div(row, 2), lax.rem(row, 2)
@@ -97,8 +102,8 @@
         pending.append(copy)
         return copy
 
-    def flush(keep):
-        while len(pending) > keep:
+    def flush():
+        while pending:
             pending.pop(0).wait_send()
 
     loads = []
@@ -141,55 +146,64 @@
     def x_chunk(half, zz):
         return xv[half, chunk_rows(zz), :]
 
+    def x_rows(half, places):
+        return jnp.concatenate([x_chunk(half, zz) for zz in places], axis=0)
+
     ag_w = None
     for it in range(ROOT_ITERS):
         mine = other = gram = None
-        for step, d in enumerate([0] + Z_ARRIVAL):
+        for step, group in enumerate([[2 * i, 2 * i + 1] for i in range(4)] if it == 0 else Z_GROUPS):
+            places = []
+            for d in group:
+                if it == 0:
+                    places.append(d)
+                else:
+                    if d:
+                        ag_w[d].wait_recv()
+                    places.append(z_at(-d))
             if it == 0:
-                zz = step
-                if step % 2 == 0:
-                    loads[step // 2].wait()
-                    loads[4 + step // 2].wait()
-            else:
-                zz = z_at(-d)
-                if d:
-                    ag_w[d].wait_recv()
-            w = rw[it, zz]
+                loads[step].wait()
+                loads[4 + step].wait()
+            w = jnp.concatenate([rw[it, zz] for zz in places], axis=1)
             high, low = parts(w)
-            other_d = nn(high, x_chunk(1, zz))
-            mine_d = nn(high, x_chunk(0, zz))
-            gram_d = gram3(high, low)
-            other = other_d if other is None else other + other_d
-            mine = mine_d if mine is None else mine + mine_d
-            gram = gram_d if gram is None else gram + gram_d
-        gram = padded(gram)
+            other = plus(other, nn(high, x_rows(1, places)))
+            mine = plus(mine, nn(high, x_rows(0, places)))
+            gram = plus(gram, gram3(high, low))
         if it == 0:
             load_rc.wait()
             load_cc.wait()
             pl.semaphore_wait(barrier, 1 + len(XY) + len(Z_SEND))
-        rxs[it, :, 0:HALF] = other
-        rxs[it, :, HALF:] = gram
+        rxs[it] = other
         swap = send(rxs.at[it], rxr.at[it], s_rx.at[it], r_rx.at[it], partner)
-        flush(1)
+        own_g = gfr.at[it, p]
+        gfr[it, p] = padded(gram)
+        gcopies = [
+            send(own_g, own_g, s_gf.at[it, i], r_gf.at[it, i], xy_peer(o)) for i, o in enumerate(XY)
+        ]
         swap.wait_recv()
-        fr[it, p, :, 0:HALF] = mine + rxr[it, :, 0:HALF]
-        fr[it, p, :, HALF:] = gram + rxr[it, :, HALF:]
+        fr[it, p] = mine + rxr[it]
         copies = [
             send(fr.at[it, p], fr.at[it, p], s_fr.at[it, i], r_fr.at[it, i], xy_peer(o))
             for i, o in enumerate(XY)
         ]
-        flush(len(copies))
+        for i in XY_ARRIVAL:
+            gcopies[i].wait_recv()
+        gram = gfr[it, 0]
+        for q in range(1, CHIPS):
+            gram = gram + gfr[it, q]
+        gfs[it] = gram
+        swap = send(gfs.at[it], gft.at[it], s_gt.at[it], r_gt.at[it], partner)
+        swap.wait_recv()
+        gram = gram + gft[it]
+        lower = small_product(gram[:, 0:K_ROOT], rh[it, 0], K_ROOT)
         for i in XY_ARRIVAL:
             copies[i].wait_recv()
         total = fr[it, 0]
         for q in range(1, CHIPS):
             total = total + fr[it, q]
-        h = rh[it, 0]
-        lower = small_product(total[:, HALF : HALF + K_ROOT], h, K_ROOT)
-        h = h * total[:, 0:HALF] / lower
+        h = rh[it, 0] * total / lower
         rh[it + 1, 0] = h
         swap = send(rh.at[it + 1, 0], rh.at[it + 1, 1], s_rh.at[it], r_rh.at[it], partner)
-        flush(1)
         high, low = parts(h)
         owns = {d: nt(high, x_chunk(0, z_at(d))) for d in Z_SEND + [0]}
         gram = gram3(high, low)
@@ -202,7 +216,6 @@
             zs_r[it, d, :, CHUNK:] = gram
             if d:
                 copies[d] = send(zs_r.at[it, d], zr_r.at[it, d], s_zr.at[it, d], r_zr.at[it, d], z_peer(d))
-        flush(len(copies))
         total = zs_r[it, 0]
         for d in Z_ARRIVAL:
             copies[d].wait_recv()
@@ -232,22 +245,29 @@
         return out
 
     for it in range(CHILD_ITERS):
-        order = [0] + Z_ARRIVAL
-        for d in order:
-            zz = z_at(-d)
-            if d:
-                ag_w[d].wait_recv()
-            if it == 0:
-                label = lb[zz, 0:K_ROOT]
-                ids = lax.broadcasted_iota(jnp.int32, (K_ROOT, CHUNK), 0)
-                own_weight = jnp.sum(jnp.where(label == ids, rw[ROOT_ITERS, zz], 0.0), axis=0, keepdims=True)
-                w = crv[zz] * own_weight
-                cw[0, zz] = w
-            else:
-                w = cw[it, zz]
-            high, low = parts(spread_of(zz, w))
-            first, last = d == 0, d == order[-1]
-            numer = nn(high, x_chunk(1, zz))
+        for group in Z_GROUPS:
+            places, ws, spreads = [], [], []
+            for d in group:
+                zz = z_at(-d)
+                if d:
+                    ag_w[d].wait_recv()
+                if it == 0:
+                    label = lb[zz, 0:K_ROOT]
+                    ids = lax.broadcasted_iota(jnp.int32, (K_ROOT, CHUNK), 0)
+                    own_weight = jnp.sum(
+                        jnp.where(label == ids, rw[ROOT_ITERS, zz], 0.0), axis=0, keepdims=True
+                    )
+                    w = crv[zz] * own_weight
+                    cw[0, zz] = w
+                else:
+                    w = cw[it, zz]
+                places.append(zz)
+                ws.append(w)
+                spreads.append(spread_of(zz, w))
+            high, low = parts(jnp.concatenate(spreads, axis=1))
+            w = jnp.concatenate(ws, axis=1)
+            first, last = group is Z_GROUPS[0], group is Z_GROUPS[-1]
+            numer = nn(high, x_rows(1, places))
             nps[it] = numer if first else nps[it] + numer
             if last:
                 swap = send(nps.at[it], cxr.at[it], s_cx.at[it, 0], r_cx.at[it, 0], partner)
@@ -265,9 +285,8 @@
                     gcopies.append(
                         send(gcs.at[it, rows], gcr.at[it, i], s_gc.at[it, i], r_gc.at[it, i], xy_peer(o))
                     )
-            numer = nn(high, x_chunk(0, zz))
+            numer = nn(high, x_rows(0, places))
             no[...] = numer if first else no[...] + numer
-        flush(1 + len(gcopies))
         swap.wait_recv()
         copies = []
         for i, o in enumerate(XY):
@@ -282,7 +301,6 @@
             gram = gram + gcr[it, i]
         gxs[it, 0] = gram
         swap_g = send(gxs.at[it, 0], gxr.at[it, 0], s_cx.at[it, 1], r_cx.at[it, 1], partner)
-        flush(len(copies) + 1)
         swap_g.wait_recv()
         gram = gram + gxr[it, 0]
         old16 = hb[it, 0, own16, :]
@@ -296,7 +314,6 @@
             send(own_h, own_h, s_ag.at[it, i], r_ag.at[it, i], xy_peer(o)) for i, o in enumerate(XY)
         ]
         relays = [send(own_h, hb.at[it + 1, 1, own8], s_re.at[it, 15], r_re.at[it, 15], partner)]
-        flush(len(copies) + 1)
         for i in XY_ARRIVAL:
             copies[i].wait_recv()
             dx, dy = XY[i]
@@ -313,7 +330,6 @@
         }
         for d in Z_SEND + [0]:
             acc[d] = nt(hbb[0], x_chunk(0, z_at(d)))
-        flush(len(relays) + len(gcopies))
         for relay in relays:
             relay.wait_recv()
         hbb[1] = hb[it + 1, 1].astype(BF16)
@@ -334,7 +350,6 @@
             gram = gram + ghr[it, d]
         gxs[it, 1:3] = gram.reshape(2, 8, TOTAL)
         swap_g = send(gxs.at[it, 1:3], gxr.at[it, 1:3], s_gx.at[it], r_gx.at[it], partner)
-        flush(len(copies) + 1)
         w = cw[it, z]
         s_high, s_low = parts(spread_of(z, w))
         swap_g.wait_recv()
@@ -364,7 +379,7 @@
     for i in range(ZN):
         put(rw.at[ROOT_ITERS, i], o_rw.at[:, i * CHUNK : (i + 1) * CHUNK])
     put(cw.at[CHILD_ITERS, z], o_cw.at[:, chunk_rows(z)])
-    flush(0)
+    flush()
     for d in Z_ARRIVAL:
         ag_w[d].wait_recv()
         put(cw.at[CHILD_ITERS, z_at(-d)], o_cw.at[:, chunk_rows(z_at(-d))])
@@ -400,7 +415,8 @@
         v(ZN, K_CHILD, CHUNK), v(r + 1, 2, K_ROOT, HALF), v(r + 1, ZN, K_ROOT, CHUNK),
         v(c + 1, ZN, K_CHILD, CHUNK), v(c + 1, 2, TOTAL, HALF), v(2, TOTAL, HALF, dtype=BF16),
         v(ZN, TOTAL, CHUNK), v(TOTAL, HALF), v(2 * TOTAL, 2 * K_CHILD),
-        v(r, K_ROOT, HALF + 128), v(r, K_ROOT, HALF + 128), v(r, CHIPS, K_ROOT, HALF + 128),
+        v(r, K_ROOT, HALF), v(r, K_ROOT, HALF), v(r, CHIPS, K_ROOT, HALF),
+        v(r, CHIPS, K_ROOT, 128), v(r, K_ROOT, 128), v(r, K_ROOT, 128),
         v(r, ZN, K_ROOT, CHUNK + 128), v(r, ZN, K_ROOT, CHUNK + 128),
         v(c, TOTAL, HALF), v(c, TOTAL, HALF), v(c, 3, 8, TOTAL), v(c, 3, 8, TOTAL),
         v(c, CHIPS, 8, HALF), v(c, n, 8, HALF),
@@ -412,6 +428,7 @@
         dma((c, 2)), dma((c, 2)), dma((c, n)), dma((c, n)), dma((c, n)), dma((c, n)),
         dma((c, n + 1)), dma((c, n + 1)), dma((c, ZN)), dma((c, ZN)), dma((c, ZN)), dma((c, ZN)),
         dma((c, n)), dma((c, n)), dma((c, ZN)), dma((c, ZN)), dma((c,)), dma((c,)),
+        dma((r, n)), dma((r, n)), dma((r,)), dma((r,)),
     ]
     shapes = (
         jax.ShapeDtypeStruct((K_ROOT, NODES), F32),

time: 139 us -> 137 us (0.986)
  Pallas kernels: 138 us -> 136 us
    pallas_call x1, Pallas kernels: 136 us -> 134 us  [body(): pl.pallas_call(kernel, out_shape=shapes, in_specs=[hbm, vmem, vmem, hbm,...]
where the time goes in v4:
time: 137 us
  Pallas kernels  136 us (99%)
    pallas_call x1, Pallas kernels, body(): pl.pallas_call(kernel, out_shape=shapes, in_specs=[hbm, vmem, vmem, hbm,...  134 us

profile of v4, /device:TPU:1, one launch (start us, length us, event | category | flops | bytes accessed | tf_op | source)
XLA Modules:
  0.0 137.0 jit_solution(4579930650460223869)
XLA Ops:
  0.6 134.1 %nmf.1 = (f32[8,2048]{1,0:T(8,128)}, f32[8,1024]{1,0:T(8,128)}, f32[16,2048]{1,0:T(8,128)}, f32[128,1024]{1,0:T(8,128)}) custom-call(bf16[2048,1024]{1,0:T(8,128)(2,1)} %x_hbm.1, s32[1,2048]{1,0:T(1,128)} %bitcast.1, f32[8,2048]{1,0:T(8,128)} %rr_ref.1, f32[8,1024]{1,0:T(8,128)} %rc_hbm.1, f32[16,2048]{1,0:T(8,128)} %cr_ref.1, f32[128,1024]{1,0:T(8,128)} %cc_hbm.1), custom_call_target="tpu_custom_call" | custom-call | tf_op jit(solution)/shard_map/nmf/pallas_call | solution.py:439
  134.8 2.0 %put_out.1 = (f32[8,2048]{1,0:T(8,128)}, f32[8,1024]{1,0:T(8,128)}, f32[16,2048]{1,0:T(8,128)}, f32[128,1024]{1,0:T(8,128)}) custom-call(f32[8,2048]{1,0:T(8,128)} %get-tuple-element.8.refs_0_, f32[8,1024]{1,0:T(8,128)} %get-tuple-element.9.refs_1_, f32[16,2048]{1,0:T(8,128)} %get-tuple-element.10.refs_2_, f32[128,1024]{1,0:T(8,128)} %get-tuple-element.11.refs_3_), custom_call_target="tpu_custom_call" | custom-call | tf_op jit(solution)/shard_map/put_out/pallas_call | solution.py:450

commit v5 on v4

--- a/solution.py
+++ b/solution.py
@@ -66,12 +66,12 @@
     x_hbm, lab_ref, rr_ref, rc_hbm, cr_ref, cc_hbm,
     o_rw, o_rh, o_cw, o_ch,
     xv, cc, lb, crv, rh, rw, cw, hb, hbb, acc, no, gacc,
-    rxs, rxr, fr, gfr, gfs, gft, zs_r, zr_r,
+    rxs, rxr, fr, gfr, gfs, gft, ghr_own, ghr_in, gzs, gzt, zs_r, zr_r,
     nps, cxr, gxs, gxr, rss, rsr, zs_c, zr_c, gcs, gcr, ghs, ghr,
     in_sem, out_sem,
     s_rx, r_rx, s_fr, r_fr, s_rh, r_rh, s_zr, r_zr, s_rw, r_rw,
     s_cx, r_cx, s_rs, r_rs, s_ag, r_ag, s_re, r_re, s_zc, r_zc, s_cw, r_cw,
-    s_gc, r_gc, s_gh, r_gh, s_gx, r_gx, s_gf, r_gf, s_gt, r_gt,
+    s_gc, r_gc, s_gh, r_gh, s_gx, r_gx, s_gf, r_gf, s_gt, r_gt, s_gz, r_gz,
 ):
     row, z = lax.axis_index("row"), lax.axis_index("col")
     p, core = lax.div(row, 2), lax.rem(row, 2)
@@ -192,7 +192,7 @@
         for q in range(1, CHIPS):
             gram = gram + gfr[it, q]
         gfs[it] = gram
-        swap = send(gfs.at[it], gft.at[it], s_gt.at[it], r_gt.at[it], partner)
+        swap = send(gfs.at[it], gft.at[it], s_gt.at[it, 0], r_gt.at[it, 0], partner)
         swap.wait_recv()
         gram = gram + gft[it]
         lower = small_product(gram[:, 0:K_ROOT], rh[it, 0], K_ROOT)
@@ -205,24 +205,33 @@
         rh[it + 1, 0] = h
         swap = send(rh.at[it + 1, 0], rh.at[it + 1, 1], s_rh.at[it], r_rh.at[it], partner)
         high, low = parts(h)
+        ghr_own[it] = padded(gram3(high, low))
+        gcopies = {
+            d: send(ghr_own.at[it], ghr_in.at[it, d], s_gz.at[it, d], r_gz.at[it, d], z_peer(d)) for d in Z_SEND
+        }
         owns = {d: nt(high, x_chunk(0, z_at(d))) for d in Z_SEND + [0]}
-        gram = gram3(high, low)
         swap.wait_recv()
-        high, low = parts(rh[it + 1, 1])
-        gram = padded(gram + gram3(high, low))
+        high = rh[it + 1, 1].astype(BF16)
         copies = {}
         for d in Z_SEND + [0]:
-            zs_r[it, d, :, 0:CHUNK] = owns[d] + nt(high, x_chunk(1, z_at(d)))
-            zs_r[it, d, :, CHUNK:] = gram
+            zs_r[it, d] = owns[d] + nt(high, x_chunk(1, z_at(d)))
             if d:
                 copies[d] = send(zs_r.at[it, d], zr_r.at[it, d], s_zr.at[it, d], r_zr.at[it, d], z_peer(d))
+        gram = ghr_own[it]
+        for d in Z_ARRIVAL:
+            gcopies[d].wait_recv()
+            gram = gram + ghr_in[it, d]
+        gzs[it] = gram
+        swap = send(gzs.at[it], gzt.at[it], s_gt.at[it, 1], r_gt.at[it, 1], partner)
+        swap.wait_recv()
+        gram = gram + gzt[it]
+        w = rw[it, z]
+        lower = small_product(gram[:, 0:K_ROOT], w, K_ROOT)
         total = zs_r[it, 0]
         for d in Z_ARRIVAL:
             copies[d].wait_recv()
             total = total + zr_r[it, d]
-        w = rw[it, z]
-        lower = small_product(total[:, CHUNK : CHUNK + K_ROOT], w, K_ROOT)
-        rw[it + 1, z] = w * total[:, 0:CHUNK] / lower
+        rw[it + 1, z] = w * total / lower
         ag_w = {
             d: send(rw.at[it + 1, z], rw.at[it + 1, z], s_rw.at[it, d], r_rw.at[it, d], z_peer(d))
             for d in Z_SEND
@@ -417,7 +426,8 @@
         v(ZN, TOTAL, CHUNK), v(TOTAL, HALF), v(2 * TOTAL, 2 * K_CHILD),
         v(r, K_ROOT, HALF), v(r, K_ROOT, HALF), v(r, CHIPS, K_ROOT, HALF),
         v(r, CHIPS, K_ROOT, 128), v(r, K_ROOT, 128), v(r, K_ROOT, 128),
-        v(r, ZN, K_ROOT, CHUNK + 128), v(r, ZN, K_ROOT, CHUNK + 128),
+        v(r, K_ROOT, 128), v(r, ZN, K_ROOT, 128), v(r, K_ROOT, 128), v(r, K_ROOT, 128),
+        v(r, ZN, K_ROOT, CHUNK), v(r, ZN, K_ROOT, CHUNK),
         v(c, TOTAL, HALF), v(c, TOTAL, HALF), v(c, 3, 8, TOTAL), v(c, 3, 8, TOTAL),
         v(c, CHIPS, 8, HALF), v(c, n, 8, HALF),
         v(c, ZN, K_CHILD, CHUNK), v(c, ZN, K_CHILD, CHUNK),
@@ -428,7 +438,7 @@
         dma((c, 2)), dma((c, 2)), dma((c, n)), dma((c, n)), dma((c, n)), dma((c, n)),
         dma((c, n + 1)), dma((c, n + 1)), dma((c, ZN)), dma((c, ZN)), dma((c, ZN)), dma((c, ZN)),
         dma((c, n)), dma((c, n)), dma((c, ZN)), dma((c, ZN)), dma((c,)), dma((c,)),
-        dma((r, n)), dma((r, n)), dma((r,)), dma((r,)),
+        dma((r, n)), dma((r, n)), dma((r, 2)), dma((r, 2)), dma((r, ZN)), dma((r, ZN)),
     ]
     shapes = (
         jax.ShapeDtypeStruct((K_ROOT, NODES), F32),

time: 137 us -> 136 us (level)
  no operation moved by 1% of the time
where the time goes in v5:
time: 136 us
  Pallas kernels  135 us (99%)
    pallas_call x1, Pallas kernels, body(): pl.pallas_call(kernel, out_shape=shapes, in_specs=[hbm, vmem, vmem, hbm,...  133 us

profile of v5, /device:TPU:1, one launch (start us, length us, event | category | flops | bytes accessed | tf_op | source)
XLA Modules:
  0.0 135.8 jit_solution(12063739190017352704)
XLA Ops:
  0.6 132.9 %nmf.1 = (f32[8,2048]{1,0:T(8,128)}, f32[8,1024]{1,0:T(8,128)}, f32[16,2048]{1,0:T(8,128)}, f32[128,1024]{1,0:T(8,128)}) custom-call(bf16[2048,1024]{1,0:T(8,128)(2,1)} %x_hbm.1, s32[1,2048]{1,0:T(1,128)} %bitcast.1, f32[8,2048]{1,0:T(8,128)} %rr_ref.1, f32[8,1024]{1,0:T(8,128)} %rc_hbm.1, f32[16,2048]{1,0:T(8,128)} %cr_ref.1, f32[128,1024]{1,0:T(8,128)} %cc_hbm.1), custom_call_target="tpu_custom_call" | custom-call | tf_op jit(solution)/shard_map/nmf/pallas_call | solution.py:449
  133.6 2.0 %put_out.1 = (f32[8,2048]{1,0:T(8,128)}, f32[8,1024]{1,0:T(8,128)}, f32[16,2048]{1,0:T(8,128)}, f32[128,1024]{1,0:T(8,128)}) custom-call(f32[8,2048]{1,0:T(8,128)} %get-tuple-element.8.refs_0_, f32[8,1024]{1,0:T(8,128)} %get-tuple-element.9.refs_1_, f32[16,2048]{1,0:T(8,128)} %get-tuple-element.10.refs_2_, f32[128,1024]{1,0:T(8,128)} %get-tuple-element.11.refs_3_), custom_call_target="tpu_custom_call" | custom-call | tf_op jit(solution)/shard_map/put_out/pallas_call | solution.py:460

commit v6 on v5

--- a/solution.py
+++ b/solution.py
@@ -26,7 +26,7 @@
 XY_ARRIVAL = list(reversed(range(len(XY))))
 Z_SEND = [4, 3, 5, 2, 6, 1, 7]
 Z_ARRIVAL = [1, 7, 2, 6, 3, 5, 4]
-Z_GROUPS = [[0], [1, 7], [2, 6], [3, 5], [4]]
+Z_GROUPS = [[0], [1, 7], [2, 6], [3, 5, 4]]
 
 
 def nn(a, b):
@@ -398,8 +398,16 @@
 
 def put_out(*refs):
     sources, targets, held, sem = refs[:4], refs[4:8], refs[8:12], refs[12]
-    loads = [pltpu.make_async_copy(s, h, sem.at[i]) for i, (s, h) in enumerate(zip(sources, held))]
-    stores = [pltpu.make_async_copy(h, t, sem.at[4 + i]) for i, (h, t) in enumerate(zip(held, targets))]
+    pieces = [(3, slice(i * 32, (i + 1) * 32)) for i in range(4)]
+    pieces += [(2, slice(0, K_CHILD)), (0, slice(0, K_ROOT)), (1, slice(0, K_ROOT))]
+    loads = [
+        pltpu.make_async_copy(sources[a].at[rows], held[a].at[rows], sem.at[i])
+        for i, (a, rows) in enumerate(pieces)
+    ]
+    stores = [
+        pltpu.make_async_copy(held[a].at[rows], targets[a].at[rows], sem.at[7 + i])
+        for i, (a, rows) in enumerate(pieces)
+    ]
     for load in loads:
         load.start()
     for load, store in zip(loads, stores):
@@ -462,7 +470,7 @@
         out_shape=shapes,
         in_specs=[hbm] * 4,
         out_specs=(hbm,) * 4,
-        scratch_shapes=[v(*s.shape) for s in shapes] + [dma((8,))],
+        scratch_shapes=[v(*s.shape) for s in shapes] + [dma((14,))],
         compiler_params=pltpu.CompilerParams(vmem_limit_bytes=63 * 1024 * 1024),
         name="put_out",
     )(*outs)

time: 136 us -> 137 us (level)
  no operation moved by 1% of the time
where the time goes in v6:
time: 137 us
  Pallas kernels  136 us (99%)
    pallas_call x1, Pallas kernels, body(): pl.pallas_call(kernel, out_shape=shapes, in_specs=[hbm, vmem, vmem, hbm,...  134 us

profile of v6, /device:TPU:1, one launch (start us, length us, event | category | flops | bytes accessed | tf_op | source)
XLA Modules:
  0.0 136.8 jit_solution(11087562008739699358)
XLA Ops:
  0.6 134.1 %nmf.1 = (f32[8,2048]{1,0:T(8,128)}, f32[8,1024]{1,0:T(8,128)}, f32[16,2048]{1,0:T(8,128)}, f32[128,1024]{1,0:T(8,128)}) custom-call(bf16[2048,1024]{1,0:T(8,128)(2,1)} %x_hbm.1, s32[1,2048]{1,0:T(1,128)} %bitcast.1, f32[8,2048]{1,0:T(8,128)} %rr_ref.1, f32[8,1024]{1,0:T(8,128)} %rc_hbm.1, f32[16,2048]{1,0:T(8,128)} %cr_ref.1, f32[128,1024]{1,0:T(8,128)} %cc_hbm.1), custom_call_target="tpu_custom_call" | custom-call | tf_op jit(solution)/shard_map/nmf/pallas_call | solution.py:457
  134.7 2.0 %put_out.1 = (f32[8,2048]{1,0:T(8,128)}, f32[8,1024]{1,0:T(8,128)}, f32[16,2048]{1,0:T(8,128)}, f32[128,1024]{1,0:T(8,128)}) custom-call(f32[8,2048]{1,0:T(8,128)} %get-tuple-element.8.refs_0_, f32[8,1024]{1,0:T(8,128)} %get-tuple-element.9.refs_1_, f32[16,2048]{1,0:T(8,128)} %get-tuple-element.10.refs_2_, f32[128,1024]{1,0:T(8,128)} %get-tuple-element.11.refs_3_), custom_call_target="tpu_custom_call" | custom-call | tf_op jit(solution)/shard_map/put_out/pallas_call | solution.py:468
